TPU v7x, 32 devices: a whole 2x2x4 slice. The times are simulated.
32 devices in a mesh: pipe: 4 (over y, x), dp: 8 (over z, core).
Axes of the slice: x: 2, y: 2, z: 4, core: 2. Of those that a mesh axis runs over, the one named last changes fastest.
Arguments:
- cotangent: bfloat16 [4, 1024, 6144], P('pipe', 'dp'), may hold values from -0.29882812 to 0.29882812
- slot_token: int32 [4, 8, 24], P('pipe', 'dp'), may hold values from 0 to 127, as said below
- slot_count: int32 [4, 8], P('pipe', 'dp'), may hold values from 6 to 24, as said below
- slot_weight: float32 [4, 8, 24], P('pipe', 'dp'), may hold values from 0.1 to 0.9
- hidden: bfloat16 [4, 8, 24, 8192], P('pipe', 'dp'), may hold values from -6 to 6
Outputs:
- down_grad: bfloat16 [4, 8192, 6144], P('pipe', 'dp')
Inputs may be any that keep to these rules, and one draw needn't show every extreme that they name: `slot_token`: within one device's 24 slots of a section the token indices are distinct. `slot_count`: in every section some device has all 24 slots live.
All inputs are finite; a program needn't handle non-finite values.
Results may differ from a plain program's by a relative error of at most 0.0049.
Values may be sent and summed in bfloat16 or wider, within the bound.
No kernel may reach another device: no remote copies, remote signals or barrier semaphores. Data moves between devices by JAX's collectives and lax.ppermute only.
A program may use at most 128 MiB of HBM per device.

v0:
```python
import jax
import jax.numpy as jnp
from jax import lax
from jax.sharding import PartitionSpec as P


def shifted(value, axis, steps):
    count = lax.axis_size(axis)
    pairs = [(source, (source + steps) % count) for source in range(count)]
    return lax.ppermute(value, axis, pairs)


def select_rows(table, positions):
    return jnp.take(table[0], positions.reshape(-1), axis=0)


def local(cotangent, slot_token, slot_count, slot_weight, hidden):
    slots = slot_token.shape[2]
    slot_pos = lax.broadcasted_iota(jnp.int32, (slots,), 0)
    live_mask = (slot_pos < slot_count[0, 0]).astype(jnp.float32)
    ahead_tokens = shifted(slot_token, "pipe", 1)
    prepared = select_rows(cotangent, ahead_tokens)
    picked = shifted(prepared, "pipe", -1)
    factors = slot_weight[0, 0] * live_mask
    scaled_rows = (factors[:, None] * picked.astype(jnp.float32)).astype(jnp.bfloat16)[None]
    exchanged = lax.all_to_all(hidden, "dp", split_axis=3, concat_axis=1, tiled=True)[0]
    gathered = lax.all_gather(scaled_rows, "dp", axis=0, tiled=True)
    width = gathered.shape[2]
    flat_rows = gathered.reshape(-1, width)
    flat_hidden = exchanged.reshape(-1, exchanged.shape[2])
    summed = lax.dot_general(
        flat_hidden, flat_rows, (((0,), (0,)), ((), ())), preferred_element_type=jnp.float32
    )
    return summed.astype(jnp.bfloat16)[None]


def solution(mesh):
    placed = (
        P("pipe", "dp", None),
        P("pipe", "dp", None),
        P("pipe", "dp"),
        P("pipe", "dp", None),
        P("pipe", "dp", None, None),
    )
    return jax.shard_map(
        local, mesh=mesh, in_specs=placed, out_specs=P("pipe", "dp", None), check_vma=False
    )
```

profile of v0, /device:TPU:0, one launch (start us, length us, event | category | flops | bytes accessed | tf_op | source)
XLA Modules:
  0.0 143.8 jit_solution(2741923419532207530)
XLA Ops:
  6.5 0.0 copy-start
  6.5 0.0 all-gather.3.cloned.1.call-start
  6.5 3.0 %collective-permute-start = (s32[1,1,24]{2,1,0:T(1,128)}, s32[1,1,24]{2,1,0:T(1,128)S(1)}, u32[]{:S(2)}, u32[]{:S(2)}) collective-permute-start(s32[1,1,24]{2,1,0:T(1,128)} %param.6), channel_id=1, source_target_pairs={{0,8},{8,16},{16,24},{24,0},{1,9},{9,17},{17,25},{25,1},{2,10},{10... | collective-permute-start | bytes 296 | tf_op jit(solution)/shard_map/ppermute | solution.py:10
  9.6 2.6 %collective-permute-done = s32[1,1,24]{2,1,0:T(1,128)S(1)} collective-permute-done((s32[1,1,24]{2,1,0:T(1,128)}, s32[1,1,24]{2,1,0:T(1,128)S(1)}, u32[]{:S(2)}, u32[]{:S(2)}) %collective-permute-start) | collective-permute-done | bytes 128 | tf_op jit(solution)/shard_map/ppermute | solution.py:10
  12.2 0.0 copy-done
  12.2 0.7 gather_fusion
  13.0 0.1 broadcast_select_fusion
  13.1 2.1 %collective-permute-start.1 = (bf16[24,6144]{1,0:T(8,128)(2,1)S(1)}, bf16[24,6144]{1,0:T(8,128)(2,1)S(1)}, u32[]{:S(2)}, u32[]{:S(2)}) collective-permute-start(bf16[24,6144]{1,0:T(8,128)(2,1)S(1)} %broadcast_select_fusion), channel_id=1, source_target_pairs={{0,24},{8,0},{16,8},{24,16},{1,25},{9,1},{17,9},{25,17},{2,26},{10... | collective-permute-start | bytes 884744 | tf_op jit(solution)/shard_map/ppermute | solution.py:10
  15.8 5.2 %collective-permute-done.1 = bf16[24,6144]{1,0:T(8,128)(2,1)S(1)} collective-permute-done((bf16[24,6144]{1,0:T(8,128)(2,1)S(1)}, bf16[24,6144]{1,0:T(8,128)(2,1)S(1)}, u32[]{:S(2)}, u32[]{:S(2)}) %collective-permute-start.1) | collective-permute-done | bytes 294944 | tf_op jit(solution)/shard_map/ppermute | solution.py:10
  21.0 0.8 multiply_convert_fusion
  21.8 0.0 all-gather.3.cloned.1.call-update
  21.9 0.0 copy-done.1
  21.9 6.7 %copy.10 = bf16[1,1,24,8192]{2,1,0,3:T(2,128)(2,1)} copy(bf16[1,1,24,8192]{3,2,1,0:T(8,128)(2,1)S(1)} %copy-done.1) | data formatting | bytes 786432 | tf_op args[4]
  28.5 0.6 broadcast.49
  29.1 46.6 %reduce = bf16[8192,24]{1,0:T(8,128)(2,1)} reduce(bf16[8192,1,1,24]{3,2,1,0:T(2,128)(2,1)} %bitcast.28, bf16[]{:T(256)} %broadcast.49), dimensions={1,2}, to_apply=%bitcast.22.reduce_sub_computation | reduce | bytes 786434
  75.6 3.9 %reshape.65 = bf16[8,2,12288]{2,1,0:T(2,128)(2,1)S(1)} reshape(bf16[8192,24]{1,0:T(8,128)(2,1)} %reduce) | data formatting | bytes 786432
  79.6 17.4 %all_to_all.15 = bf16[8,2,12288]{2,1,0:T(2,128)(2,1)S(1)} all-to-all(bf16[8,2,12288]{2,1,0:T(2,128)(2,1)S(1)} %reshape.65), channel_id=1, replica_groups=mesh['pipe'=4,'dp'=8] {'dp'}, dimensions={0} | all-to-all | bytes 786432 | tf_op jit(solution)/shard_map/all_to_all | solution.py:26
  96.9 6.6 %reshape.66 = bf16[8192,1,1,24]{3,2,1,0:T(2,128)(2,1)} reshape(bf16[8,2,12288]{2,1,0:T(2,128)(2,1)S(1)} %all_to_all.15) | data formatting | bytes 786432
  103.6 8.0 %copy.11 = bf16[1,1,24,8192]{3,2,1,0:T(8,128)(2,1)S(1)} copy(bf16[1,1,24,8192]{2,1,0,3:T(2,128)(2,1)} %bitcast.29) | data formatting | bytes 786432 | tf_op jit(solution)/shard_map/all_to_all | solution.py:26
  111.6 0.2 copy.14
  111.8 0.2 copy.12
  112.1 0.0 all-gather.3.cloned.1.call-done
  112.1 8.3 %convert_bitcast_fusion = bf16[1,1024,6144]{1,2,0:T(8,128)(2,1)} fusion(bf16[192,6144]{1,0:T(8,128)(2,1)} %all-gather.3.cloned.1.call-done, bf16[192,1024]{1,0:T(8,128)(2,1)S(1)} %bitcast.32), kind=kOutput, calls=%fused_computation.1 | convolution fusion | flops 2422210560 | bytes 15335424 | tf_op jit(solution)/shard_map/dot_general | solution.py:31
  120.4 16.6 %copy.13 = bf16[1,1024,6144]{2,1,0:T(8,128)(2,1)} copy(bf16[1,1024,6144]{1,2,0:T(8,128)(2,1)} %convert_bitcast_fusion) | data formatting | bytes 25165824 | tf_op jit(solution)/shard_map/broadcast_in_dim | solution.py:34
  (7 shorter events, 0.0 us)
Async XLA Ops:
  6.5 5.7 %copy-start = (bf16[1,128,6144]{2,1,0:T(8,128)(2,1)S(1)}, bf16[1,128,6144]{2,1,0:T(8,128)(2,1)}, u32[]{:S(2)}) copy-start(bf16[1,128,6144]{2,1,0:T(8,128)(2,1)} %param.5) | copy-start | bytes 4718596
  6.5 9.3 %copy-start.2 = (f32[1,1,24]{2,1,0:T(1,128)S(1)}, f32[1,1,24]{2,1,0:T(1,128)}, u32[]{:S(2)}) copy-start(f32[1,1,24]{2,1,0:T(1,128)} %param.8) | copy-start | bytes 292
  6.5 15.3 %copy-start.1 = (bf16[1,1,24,8192]{3,2,1,0:T(8,128)(2,1)S(1)}, bf16[1,1,24,8192]{3,2,1,0:T(8,128)(2,1)}, u32[]{:S(2)}) copy-start(bf16[1,1,24,8192]{3,2,1,0:T(8,128)(2,1)} %param.9) | copy-start | bytes 1179652
  6.5 105.5 %all-gather.3.cloned.1.call-start = ((), (), s32[]{:S(2)}) async-start(), calls=%async_computation.1 | async-start | bytes 2654208 | tf_op jit(solution)/shard_map/all_gather | solution.py:27
  6.5 5.7 %collective-permute-start = (s32[1,1,24]{2,1,0:T(1,128)}, s32[1,1,24]{2,1,0:T(1,128)S(1)}, u32[]{:S(2)}, u32[]{:S(2)}) collective-permute-start(s32[1,1,24]{2,1,0:T(1,128)} %param.6), channel_id=1, source_target_pairs={{0,8},{8,16},{16,24},{24,0},{1,9},{9,17},{17,25},{25,1},{2,10},{10... | collective-permute-start | bytes 296 | tf_op jit(solution)/shard_map/ppermute | solution.py:10
  13.1 7.9 %collective-permute-start.1 = (bf16[24,6144]{1,0:T(8,128)(2,1)S(1)}, bf16[24,6144]{1,0:T(8,128)(2,1)S(1)}, u32[]{:S(2)}, u32[]{:S(2)}) collective-permute-start(bf16[24,6144]{1,0:T(8,128)(2,1)S(1)} %broadcast_select_fusion), channel_id=1, source_target_pairs={{0,24},{8,0},{16,8},{24,16},{1,25},{9,1},{17,9},{25,17},{2,26},{10... | collective-permute-start | bytes 884744 | tf_op jit(solution)/shard_map/ppermute | solution.py:10
Sparse Core Ops, SparseCore 0:
  22.0 32.8 all-gather.2
where the time goes:
time: 145 us; the launch traced here: 144 us
  other arithmetic  47.5 us (33%)
  local copies, waits for them, and re-layouts  43.5 us (30%)
  blocking collectives  17.4 us (12%)
  between operations  14.1 us (10%)
  matrix products  8.29 us (6%)
  waiting for transfers between devices  7.86 us (5%)
  starting transfers between devices  5.09 us (4%)
    unnamed x1, other arithmetic  46.6 us
    unnamed x11, local copies, waits for them, and re-layouts  18 us
    all_to_all x1, blocking collectives, local(): lax.all_to_all(hidden, 'dp', split_axis=3, concat_axis=1, tiled=True)[0]  17.4 us
    broadcast_in_dim x1, local copies, waits for them, and re-layouts, local(): return summed.astype(jnp.bfloat16)[None]  16.6 us
    dot_general x1, matrix products, local(): lax.dot_general(flat_hidden, flat_rows, (((0,), (0,)), ((), ())), preferr...  8.29 us
    all_to_all x2, local copies, waits for them, and re-layouts, local(): lax.all_to_all(hidden, 'dp', split_axis=3, concat_axis=1, tiled=True)[0]  8.22 us
    ppermute x2, waiting for transfers between devices, shifted(): return lax.ppermute(value, axis, pairs)  7.82 us
    ppermute x2, starting transfers between devices, shifted(): return lax.ppermute(value, axis, pairs)  5.09 us
  transfers between devices with their start and end apart: 3, of which 2 were waited for; matrix products, arithmetic and copies ran while one was open for 51% of the time, Pallas kernels for 0%

commit v1 on v0

v1 whole, which is shorter than its diff:
```python
import jax
import jax.numpy as jnp
from jax import lax
from jax.experimental import pallas as pl
from jax.experimental.pallas import tpu as pltpu
from jax.sharding import PartitionSpec as P


CORES = 2
CHUNKS = ((7, True), (5, True))
TILE = 256

VMEM = pl.BlockSpec(memory_space=pltpu.VMEM)
SMEM = pl.BlockSpec(memory_space=pltpu.SMEM)
ANY = pl.BlockSpec(memory_space=pl.ANY)


def live_factors(count, weight):
    def kernel(count_ref, weight_ref, out):
        slot = lax.broadcasted_iota(jnp.int32, weight.shape, 1)
        out[...] = weight_ref[...] * (slot < count_ref[...]).astype(jnp.float32)

    return pl.pallas_call(
        kernel,
        in_specs=[VMEM, VMEM],
        out_specs=VMEM,
        out_shape=jax.ShapeDtypeStruct(weight.shape, weight.dtype),
        compiler_params=pltpu.CompilerParams(vmem_limit_bytes=1 << 20),
        name="live_factors",
    )(count, weight)


def split_hidden(chip, own, chips):
    slots = own.shape[0]
    units = own.shape[1] // chips

    def kernel(chip_ref, own_ref, *outs):
        for k, out in enumerate(outs):
            begin = pl.multiple_of((chip_ref[0] ^ k) * units, 128)
            out[...] = own_ref[:, pl.ds(begin, units)]

    out = jax.ShapeDtypeStruct((slots, units), own.dtype)
    return pl.pallas_call(
        kernel,
        in_specs=[SMEM, VMEM],
        out_specs=[VMEM] * chips,
        out_shape=[out] * chips,
        compiler_params=pltpu.CompilerParams(vmem_limit_bytes=4 << 20),
        name="split_hidden",
    )(chip, own)


def join_hidden(core, kept, got, chips):
    slots = kept.shape[0] // chips

    def kernel(core_ref, kept_ref, got_ref, out):
        for k in range(chips):
            own = kept_ref[k * slots : (k + 1) * slots, :]
            other = got_ref[k * slots : (k + 1) * slots, :]
            begin = 2 * k * slots
            out[begin : begin + slots, :] = jnp.where(core_ref[0] == 0, own, other)
            out[begin + slots : begin + 2 * slots, :] = jnp.where(core_ref[0] == 0, other, own)

    return pl.pallas_call(
        kernel,
        in_specs=[SMEM, VMEM, VMEM],
        out_specs=VMEM,
        out_shape=jax.ShapeDtypeStruct((2 * chips * slots, kept.shape[1]), kept.dtype),
        compiler_params=pltpu.CompilerParams(vmem_limit_bytes=4 << 20),
        name="join_hidden",
    )(core, kept, got)


def product(core, lhs, rows, out, width, half, offset):
    _, units = lhs.shape
    size = rows.shape[1]
    steps = size // TILE
    span = width // 2

    def kernel(core_ref, lhs_ref, rows_ref, *refs):
        out_ref, made, sems = refs[-3:]
        mine = core_ref[0]
        base = (mine if half == 0 else 1 - mine) * span + offset
        copies = []
        for step in range(steps):
            made[step] = lax.dot_general(
                lhs_ref[...],
                rows_ref[:, step * TILE : (step + 1) * TILE],
                (((0,), (0,)), ((), ())),
                preferred_element_type=jnp.float32,
            ).astype(made.dtype)
            begin = pl.multiple_of(base + step * TILE, TILE)
            copy = pltpu.make_async_copy(
                made.at[step], out_ref.at[:, pl.ds(begin, TILE)], sems.at[step]
            )
            copy.start()
            copies.append(copy)
        for copy in copies:
            copy.wait()

    operands = [core, lhs, rows]
    in_specs = [SMEM, VMEM, VMEM]
    aliases = {}
    if out is not None:
        aliases = {len(operands): 0}
        operands.append(out)
        in_specs.append(ANY)
    return pl.pallas_call(
        kernel,
        in_specs=in_specs,
        out_specs=ANY,
        out_shape=jax.ShapeDtypeStruct((units, width), jnp.bfloat16),
        scratch_shapes=[
            pltpu.VMEM((steps, units, TILE), jnp.bfloat16),
            pltpu.SemaphoreType.DMA((steps,)),
        ],
        input_output_aliases=aliases,
        compiler_params=pltpu.CompilerParams(vmem_limit_bytes=10 << 20),
        name="product",
    )(*operands)


def local(cotangent, slot_token, slot_count, slot_weight, hidden):
    sections, members = lax.axis_size("pipe"), lax.axis_size("dp")
    chips = members // CORES
    me = lax.axis_index("dp")
    chip, core = me // CORES, me % CORES
    place = jnp.stack([chip, core]).astype(jnp.int32)
    slots = slot_token.shape[2]
    width = cotangent.shape[2]
    span = width // 2
    first = core == 0

    def partner(value):
        return lax.ppermute(value, "dp", [(s, s ^ 1) for s in range(members)])

    def to_chip(value, pairs):
        return lax.ppermute(
            value, "dp", [(a * CORES + i, b * CORES + i) for a, b in pairs for i in range(CORES)]
        )

    def back_to(value, flip):
        pairs = [
            (s * members + d, ((s - 1) % sections) * members + (d ^ flip))
            for s in range(sections)
            for d in range(members)
        ]
        return lax.ppermute(value, ("pipe", "dp"), pairs)

    def in_order(mine, other):
        return jnp.where(first, jnp.concatenate([mine, other]), jnp.concatenate([other, mine]))

    asked = lax.ppermute(
        slot_token, "pipe", [(s, (s + 1) % sections) for s in range(sections)]
    )
    hidden_parts = list(split_hidden(place[:1], hidden[0, 0], chips))
    for k in range(1, chips):
        hidden_parts[k] = to_chip(hidden_parts[k], [(a, a ^ k) for a in range(chips)])
    came = jnp.concatenate(hidden_parts)
    units = came.shape[1] // CORES
    low, high = came[:, :units], came[:, units:]
    kept, given = jnp.where(first, low, high), jnp.where(first, high, low)
    lhs = join_hidden(place[1:2], kept, partner(given), chips)

    positions = lax.broadcasted_iota(jnp.int32, (slots, cotangent.shape[1]), 1)
    chosen = (asked[0, 0][:, None] == positions).astype(jnp.bfloat16)
    rows = jnp.dot(chosen, cotangent[0], preferred_element_type=jnp.bfloat16)
    factors = live_factors(slot_count, slot_weight[0]).reshape(slots)
    other_factors = partner(factors)
    both = in_order(factors, other_factors)[:, None]

    def at(distance, value):
        return to_chip(value, [(a, a ^ distance) for a in range(chips)])

    out, begin = None, 0
    for share, relayed in CHUNKS:
        end = begin + span * share // sum(part for part, _ in CHUNKS)
        low, high = rows[:, begin:end], rows[:, span + begin : span + end]
        mine = back_to(jnp.where(first, low, high), 0)
        other = back_to(jnp.where(first, high, low), 1)
        pair = (both * in_order(mine, other).astype(jnp.float32)).astype(jnp.bfloat16)
        parts = [pair]
        for k in range(1, chips):
            if relayed and k > 2 and chips == 4:
                parts.append(at(1, parts[2]))
            else:
                parts.append(at(k, pair))
        whole = jnp.concatenate(parts)
        rest = partner(whole)
        out = product(place[1:2], lhs, whole, out, width, 0, begin)
        out = product(place[1:2], lhs, rest, out, width, 1, begin)
        begin = end
    return out[None]


def solution(mesh):
    placed = (
        P("pipe", "dp", None),
        P("pipe", "dp", None),
        P("pipe", "dp"),
        P("pipe", "dp", None),
        P("pipe", "dp", None, None),
    )

    return jax.shard_map(
        local, mesh=mesh, in_specs=placed, out_specs=P("pipe", "dp", None), check_vma=False
    )
```

time: 145 us -> 53.7 us (0.37)
  other arithmetic: 47.5 us -> 0.41 us
  local copies, waits for them, and re-layouts: 43.5 us -> 1.68 us
  blocking collectives: 17.4 us -> 0 us
  starting transfers between devices: 5.09 us -> 20.9 us
  between operations: 14.1 us -> 0.84 us
  waiting for transfers between devices: 7.86 us -> 20.5 us
  Pallas kernels: 0 us -> 8.9 us
  matrix products: 8.29 us -> 0.36 us
    unnamed x1 -> x0, other arithmetic: 46.6 us -> none
    all_to_all x1 -> x0, blocking collectives: 17.4 us -> none  [local(): lax.all_to_all(hidden, 'dp', split_axis=3, concat_axis=1, tiled=True)[0]]
    broadcast_in_dim x1 -> x0, local copies, waits for them, and re-layouts: 16.6 us -> none  [local(): return summed.astype(jnp.bfloat16)[None]]
    unnamed x11 -> x9, local copies, waits for them, and re-layouts: 18 us -> 1.67 us
    ppermute x2 -> x18, starting transfers between devices: 5.09 us -> 20.9 us  [the longest x9 12.2 us: to_chip(): lax.ppermute(value, 'dp', [(a * CORES + i, b * CORES + i) for a, b in pai...]
    ppermute x2 -> x18, waiting for transfers between devices: 7.82 us -> 20.5 us  [the longest x9 14.1 us: to_chip(): lax.ppermute(value, 'dp', [(a * CORES + i, b * CORES + i) for a, b in pai...]
    pallas_call x0 -> x7, Pallas kernels: none -> 8.9 us  [the longest x4 8.75 us: product(): pl.pallas_call(kernel, in_specs=in_specs, out_specs=ANY, out_shape=jax.Sh...]
    all_to_all x2 -> x0, local copies, waits for them, and re-layouts: 8.22 us -> none  [local(): lax.all_to_all(hidden, 'dp', split_axis=3, concat_axis=1, tiled=True)[0]]
  transfers between devices with their start and end apart: 3 -> 18, of which waited for: 2 -> 6; matrix products, arithmetic and copies ran while one was open for 51% -> 1% of each run, Pallas kernels for 0% -> 13%
where the time goes in v1:
time: 53.7 us; the launch traced here: 53.6 us
  starting transfers between devices  20.9 us (39%)
  waiting for transfers between devices  20.5 us (38%)
  Pallas kernels  8.9 us (17%)
  local copies, waits for them, and re-layouts  1.68 us (3%)
  between operations  0.84 us (2%)
    ppermute x9, waiting for transfers between devices, to_chip(): lax.ppermute(value, 'dp', [(a * CORES + i, b * CORES + i) for a, b in pai...  14.1 us
    ppermute x9, starting transfers between devices, to_chip(): lax.ppermute(value, 'dp', [(a * CORES + i, b * CORES + i) for a, b in pai...  12.2 us
    pallas_call x4, Pallas kernels, product(): pl.pallas_call(kernel, in_specs=in_specs, out_specs=ANY, out_shape=jax.Sh...  8.75 us
    ppermute x4, starting transfers between devices, back_to(): return lax.ppermute(value, ('pipe', 'dp'), pairs)  5.08 us
    ppermute x4, waiting for transfers between devices, back_to(): return lax.ppermute(value, ('pipe', 'dp'), pairs)  4.86 us
    ppermute x1, starting transfers between devices, local(): lax.ppermute(slot_token, 'pipe', [(s, (s + 1) % sections) for s in range(...  2.97 us
    unnamed x9, local copies, waits for them, and re-layouts  1.67 us
    ppermute x4, waiting for transfers between devices, partner(): return lax.ppermute(value, 'dp', [(s, s ^ 1) for s in range(members)])  1.52 us
  transfers between devices with their start and end apart: 18, of which 6 were waited for; matrix products, arithmetic and copies ran while one was open for 1% of the time, Pallas kernels for 13%

profile of v1, /device:TPU:0, one launch (start us, length us, event | category | flops | bytes accessed | tf_op | source)
XLA Modules:
  0.0 53.6 jit_solution(13641051097139385974)
XLA Ops:
  0.0 3.0 %collective-permute-start.5 = (s32[1,1,24]{2,1,0:T(1,128)}, s32[1,1,24]{2,1,0:T(1,128)S(1)}, u32[]{:S(2)}, u32[]{:S(2)}) collective-permute-start(s32[1,1,24]{2,1,0:T(1,128)} %param.6), channel_id=1, source_target_pairs={{0,8},{8,16},{16,24},{24,0},{1,9},{9,17},{17,25},{25,1},{2,10},{10... | collective-permute-start | bytes 296 | tf_op jit(solution)/shard_map/ppermute | solution.py:153
  3.6 0.6 %copy-done.2 = f32[1,1,24]{2,1,0:T(1,128)S(1)} copy-done((f32[1,1,24]{2,1,0:T(1,128)S(1)}, f32[1,1,24]{2,1,0:T(1,128)}, u32[]{:S(2)}) %copy-start.2) | copy-done | bytes 120
  4.4 1.0 %copy-done.1 = bf16[1,1,24,8192]{3,2,1,0:T(8,128)(2,1)S(1)} copy-done((bf16[1,1,24,8192]{3,2,1,0:T(8,128)(2,1)S(1)}, bf16[1,1,24,8192]{3,2,1,0:T(8,128)(2,1)}, u32[]{:S(2)}) %copy-start.1) | copy-done | bytes 393240
  5.4 1.6 %collective-permute-start = (bf16[24,2048]{1,0:T(8,128)(2,1)S(1)}, bf16[24,2048]{1,0:T(8,128)(2,1)S(1)}, u32[]{:S(2)}, u32[]{:S(2)}) collective-permute-start(bf16[24,2048]{1,0:T(8,128)(2,1)S(1)} %get-tuple-element.10), channel_id=1, source_target_pairs={{0,2},{1,3},{2,0},{3,1},{4,6},{5,7},{6,4},{7,5},{8,10},{9,11},{10,... | collective-permute-start | bytes 294920 | tf_op jit(solution)/shard_map/ppermute | solution.py:138
  7.0 2.6 %collective-permute-start.1 = (bf16[24,2048]{1,0:T(8,128)(2,1)S(1)}, bf16[24,2048]{1,0:T(8,128)(2,1)S(1)}, u32[]{:S(2)}, u32[]{:S(2)}) collective-permute-start(bf16[24,2048]{1,0:T(8,128)(2,1)S(1)} %get-tuple-element.11), channel_id=1, source_target_pairs={{0,4},{1,5},{2,6},{3,7},{4,0},{5,1},{6,2},{7,3},{8,12},{9,13},{10,... | collective-permute-start | bytes 294920 | tf_op jit(solution)/shard_map/ppermute | solution.py:138
  10.3 1.3 %collective-permute-start.6 = (bf16[24,1280]{1,0:T(8,128)(2,1)S(1)}, bf16[24,1280]{1,0:T(8,128)(2,1)S(1)}, u32[]{:S(2)}, u32[]{:S(2)}) collective-permute-start(bf16[24,1280]{1,0:T(8,128)(2,1)S(1)} %get-tuple-element.17), channel_id=1, source_target_pairs={{0,24},{1,25},{2,26},{3,27},{4,28},{5,29},{6,30},{7,31},{8,0},{9,1... | collective-permute-start | bytes 184328 | tf_op jit(solution)/shard_map/ppermute | solution.py:148
  11.6 0.8 %collective-permute-start.7 = (bf16[24,1280]{1,0:T(8,128)(2,1)S(1)}, bf16[24,1280]{1,0:T(8,128)(2,1)S(1)}, u32[]{:S(2)}, u32[]{:S(2)}) collective-permute-start(bf16[24,1280]{1,0:T(8,128)(2,1)S(1)} %get-tuple-element.18), channel_id=1, source_target_pairs={{0,25},{1,24},{2,27},{3,26},{4,29},{5,28},{6,31},{7,30},{8,1},{9,0... | collective-permute-start | bytes 184328 | tf_op jit(solution)/shard_map/ppermute | solution.py:148
  12.5 2.1 %collective-permute-done.6 = bf16[24,1280]{1,0:T(8,128)(2,1)S(1)} collective-permute-done((bf16[24,1280]{1,0:T(8,128)(2,1)S(1)}, bf16[24,1280]{1,0:T(8,128)(2,1)S(1)}, u32[]{:S(2)}, u32[]{:S(2)}) %collective-permute-start.6) | collective-permute-done | bytes 61472 | tf_op jit(solution)/shard_map/ppermute | solution.py:148
  14.6 2.1 %collective-permute-start.12 = (bf16[24,1792]{1,0:T(8,128)(2,1)S(1)}, bf16[24,1792]{1,0:T(8,128)(2,1)S(1)}, u32[]{:S(2)}, u32[]{:S(2)}) collective-permute-start(bf16[24,1792]{1,0:T(8,128)(2,1)S(1)} %get-tuple-element.15), channel_id=1, source_target_pairs={{0,24},{1,25},{2,26},{3,27},{4,28},{5,29},{6,30},{7,31},{8,0},{9,1... | collective-permute-start | bytes 258056 | tf_op jit(solution)/shard_map/ppermute | solution.py:148
  16.7 0.8 %collective-permute-start.13 = (bf16[24,1792]{1,0:T(8,128)(2,1)S(1)}, bf16[24,1792]{1,0:T(8,128)(2,1)S(1)}, u32[]{:S(2)}, u32[]{:S(2)}) collective-permute-start(bf16[24,1792]{1,0:T(8,128)(2,1)S(1)} %get-tuple-element.16), channel_id=1, source_target_pairs={{0,25},{1,24},{2,27},{3,26},{4,29},{5,28},{6,31},{7,30},{8,1},{9,0... | collective-permute-start | bytes 258056 | tf_op jit(solution)/shard_map/ppermute | solution.py:148
  17.6 2.8 %collective-permute-done.12 = bf16[24,1792]{1,0:T(8,128)(2,1)S(1)} collective-permute-done((bf16[24,1792]{1,0:T(8,128)(2,1)S(1)}, bf16[24,1792]{1,0:T(8,128)(2,1)S(1)}, u32[]{:S(2)}, u32[]{:S(2)}) %collective-permute-start.12) | collective-permute-done | bytes 86048 | tf_op jit(solution)/shard_map/ppermute | solution.py:148
  20.4 1.5 %collective-permute-start.9 = (bf16[48,1280]{1,0:T(8,128)(2,1)S(1)}, bf16[48,1280]{1,0:T(8,128)(2,1)S(1)}, u32[]{:S(2)}, u32[]{:S(2)}) collective-permute-start(bf16[48,1280]{1,0:T(8,128)(2,1)S(1)} %multiply_convert_fusion.1), channel_id=1, source_target_pairs={{0,4},{1,5},{2,6},{3,7},{4,0},{5,1},{6,2},{7,3},{8,12},{9,13},{10,... | collective-permute-start | bytes 368648 | tf_op jit(solution)/shard_map/ppermute | solution.py:138
  21.9 2.5 %collective-permute-start.8 = (bf16[48,1280]{1,0:T(8,128)(2,1)S(1)}, bf16[48,1280]{1,0:T(8,128)(2,1)S(1)}, u32[]{:S(2)}, u32[]{:S(2)}) collective-permute-start(bf16[48,1280]{1,0:T(8,128)(2,1)S(1)} %multiply_convert_fusion.1), channel_id=1, source_target_pairs={{0,2},{1,3},{2,0},{3,1},{4,6},{5,7},{6,4},{7,5},{8,10},{9,11},{10,... | collective-permute-start | bytes 368648 | tf_op jit(solution)/shard_map/ppermute | solution.py:138
  24.5 1.6 %collective-permute-start.15 = (bf16[48,1792]{1,0:T(8,128)(2,1)S(1)}, bf16[48,1792]{1,0:T(8,128)(2,1)S(1)}, u32[]{:S(2)}, u32[]{:S(2)}) collective-permute-start(bf16[48,1792]{1,0:T(8,128)(2,1)S(1)} %multiply_convert_fusion), channel_id=1, source_target_pairs={{0,4},{1,5},{2,6},{3,7},{4,0},{5,1},{6,2},{7,3},{8,12},{9,13},{10,... | collective-permute-start | bytes 516104 | tf_op jit(solution)/shard_map/ppermute | solution.py:138
  26.2 8.8 %collective-permute-done.15 = bf16[48,1792]{1,0:T(8,128)(2,1)S(1)} collective-permute-done((bf16[48,1792]{1,0:T(8,128)(2,1)S(1)}, bf16[48,1792]{1,0:T(8,128)(2,1)S(1)}, u32[]{:S(2)}, u32[]{:S(2)}) %collective-permute-start.15) | collective-permute-done | bytes 172064 | tf_op jit(solution)/shard_map/ppermute | solution.py:138
  35.0 2.1 %collective-permute-start.10 = (bf16[48,1280]{1,0:T(8,128)(2,1)S(1)}, bf16[48,1280]{1,0:T(8,128)(2,1)S(1)}, u32[]{:S(2)}, u32[]{:S(2)}) collective-permute-start(bf16[48,1280]{1,0:T(8,128)(2,1)S(1)} %collective-permute-done.9), channel_id=1, source_target_pairs={{0,2},{1,3},{2,0},{3,1},{4,6},{5,7},{6,4},{7,5},{8,10},{9,11},{10,... | collective-permute-start | bytes 368648 | tf_op jit(solution)/shard_map/ppermute | solution.py:138
  37.1 4.1 %collective-permute-done.16 = bf16[48,1792]{1,0:T(8,128)(2,1)S(1)} collective-permute-done((bf16[48,1792]{1,0:T(8,128)(2,1)S(1)}, bf16[48,1792]{1,0:T(8,128)(2,1)S(1)}, u32[]{:S(2)}, u32[]{:S(2)}) %collective-permute-start.16) | collective-permute-done | bytes 172064 | tf_op jit(solution)/shard_map/ppermute | solution.py:138
  41.3 1.2 %collective-permute-done.10 = bf16[48,1280]{1,0:T(8,128)(2,1)S(1)} collective-permute-done((bf16[48,1280]{1,0:T(8,128)(2,1)S(1)}, bf16[48,1280]{1,0:T(8,128)(2,1)S(1)}, u32[]{:S(2)}, u32[]{:S(2)}) %collective-permute-start.10) | collective-permute-done | bytes 122912 | tf_op jit(solution)/shard_map/ppermute | solution.py:138
  42.7 0.5 %collective-permute-start.3 = (bf16[96,1024]{1,0:T(8,128)(2,1)S(1)}, bf16[96,1024]{1,0:T(8,128)(2,1)S(1)}, u32[]{:S(2)}, u32[]{:S(2)}) collective-permute-start(bf16[96,1024]{1,0:T(8,128)(2,1)S(1)} %get-tuple-element.13), channel_id=1, source_target_pairs={{0,1},{1,0},{2,3},{3,2},{4,5},{5,4},{6,7},{7,6},{8,9},{9,8},{10,11... | collective-permute-start | bytes 589832 | tf_op jit(solution)/shard_map/ppermute | solution.py:135
  43.2 1.5 %collective-permute-done.3.got_ref = bf16[96,1024]{1,0:T(8,128)(2,1)S(1)} collective-permute-done((bf16[96,1024]{1,0:T(8,128)(2,1)S(1)}, bf16[96,1024]{1,0:T(8,128)(2,1)S(1)}, u32[]{:S(2)}, u32[]{:S(2)}) %collective-permute-start.3) | collective-permute-done | bytes 196640 | tf_op jit(solution)/shard_map/ppermute | solution.py:135
  44.8 2.4 %product.4.refs_0_ = bf16[1024,6144]{1,0:T(8,128)(2,1)} custom-call(s32[1]{0:T(128)} %bitcast.core_ref, bf16[192,1024]{1,0:T(8,128)(2,1)S(1)} %join_hidden.1.lhs_ref, bf16[192,1792]{1,0:T(8,128)(2,1)S(1)} %pad_maximum_fusion.rows_ref), custom_call_target="tpu_custom_call" | custom-call | tf_op jit(solution)/shard_map/product/pallas_call | solution.py:108
  47.2 2.4 %product.5.refs_0_ = bf16[1024,6144]{1,0:T(8,128)(2,1)} custom-call(s32[1]{0:T(128)} %bitcast.core_ref, bf16[192,1024]{1,0:T(8,128)(2,1)S(1)} %join_hidden.1.lhs_ref, bf16[192,1792]{1,0:T(8,128)(2,1)S(1)} %collective-permute-done.17.rows_ref, bf16[1024,6144]{1,0:T(8,128)(2,1)} %product.4.refs_0_), custom_call_target="tpu_custom_call", output_to_operand_aliasing={{}: (3, {})} | custom-call | tf_op jit(solution)/shard_map/product/pallas_call | solution.py:108
  49.6 2.0 %product.6.refs_0_ = bf16[1024,6144]{1,0:T(8,128)(2,1)} custom-call(s32[1]{0:T(128)} %bitcast.core_ref, bf16[192,1024]{1,0:T(8,128)(2,1)S(1)} %join_hidden.1.lhs_ref, bf16[192,1280]{1,0:T(8,128)(2,1)S(1)} %pad_maximum_fusion.1.rows_ref, bf16[1024,6144]{1,0:T(8,128)(2,1)} %product.5.refs_0_), custom_call_target="tpu_custom_call", output_to_operand_aliasing={{}: (3, {})} | custom-call | tf_op jit(solution)/shard_map/product/pallas_call | solution.py:108
  51.6 2.0 %product.7 = bf16[1024,6144]{1,0:T(8,128)(2,1)} custom-call(s32[1]{0:T(128)} %bitcast.core_ref, bf16[192,1024]{1,0:T(8,128)(2,1)S(1)} %join_hidden.1.lhs_ref, bf16[192,1280]{1,0:T(8,128)(2,1)S(1)} %collective-permute-done.11.rows_ref, bf16[1024,6144]{1,0:T(8,128)(2,1)} %product.6.refs_0_), custom_call_target="tpu_custom_call", output_to_operand_aliasing={{}: (3, {})} | custom-call | tf_op jit(solution)/shard_map/product/pallas_call | solution.py:108
  (38 shorter events, 1.4 us)
Async XLA Ops:
  0.0 9.9 %copy-start = (bf16[1,128,6144]{2,1,0:T(8,128)(2,1)S(1)}, bf16[1,128,6144]{2,1,0:T(8,128)(2,1)}, u32[]{:S(2)}) copy-start(bf16[1,128,6144]{2,1,0:T(8,128)(2,1)} %param.5) | copy-start | bytes 4718596
  0.0 9.8 %collective-permute-start.5 = (s32[1,1,24]{2,1,0:T(1,128)}, s32[1,1,24]{2,1,0:T(1,128)S(1)}, u32[]{:S(2)}, u32[]{:S(2)}) collective-permute-start(s32[1,1,24]{2,1,0:T(1,128)} %param.6), channel_id=1, source_target_pairs={{0,8},{8,16},{16,24},{24,0},{1,9},{9,17},{17,25},{25,1},{2,10},{10... | collective-permute-start | bytes 296 | tf_op jit(solution)/shard_map/ppermute | solution.py:153
  3.6 0.7 %copy-start.2 = (f32[1,1,24]{2,1,0:T(1,128)S(1)}, f32[1,1,24]{2,1,0:T(1,128)}, u32[]{:S(2)}) copy-start(f32[1,1,24]{2,1,0:T(1,128)} %param.8) | copy-start | bytes 292
  4.4 7.2 %collective-permute-start.4 = (f32[24]{0:T(128)S(1)}, f32[24]{0:T(128)S(1)}, u32[]{:S(2)}, u32[]{:S(2)}) collective-permute-start(f32[24]{0:T(128)S(1)} %bitcast.11), channel_id=1, source_target_pairs={{0,1},{1,0},{2,3},{3,2},{4,5},{5,4},{6,7},{7,6},{8,9},{9,8},{10,11... | collective-permute-start | bytes 296 | tf_op jit(solution)/shard_map/ppermute | solution.py:135
  4.4 1.0 %copy-start.1 = (bf16[1,1,24,8192]{3,2,1,0:T(8,128)(2,1)S(1)}, bf16[1,1,24,8192]{3,2,1,0:T(8,128)(2,1)}, u32[]{:S(2)}) copy-start(bf16[1,1,24,8192]{3,2,1,0:T(8,128)(2,1)} %param.9) | copy-start | bytes 1179652
  5.4 19.1 %collective-permute-start = (bf16[24,2048]{1,0:T(8,128)(2,1)S(1)}, bf16[24,2048]{1,0:T(8,128)(2,1)S(1)}, u32[]{:S(2)}, u32[]{:S(2)}) collective-permute-start(bf16[24,2048]{1,0:T(8,128)(2,1)S(1)} %get-tuple-element.10), channel_id=1, source_target_pairs={{0,2},{1,3},{2,0},{3,1},{4,6},{5,7},{6,4},{7,5},{8,10},{9,11},{10,... | collective-permute-start | bytes 294920 | tf_op jit(solution)/shard_map/ppermute | solution.py:138
  7.0 19.0 %collective-permute-start.1 = (bf16[24,2048]{1,0:T(8,128)(2,1)S(1)}, bf16[24,2048]{1,0:T(8,128)(2,1)S(1)}, u32[]{:S(2)}, u32[]{:S(2)}) collective-permute-start(bf16[24,2048]{1,0:T(8,128)(2,1)S(1)} %get-tuple-element.11), channel_id=1, source_target_pairs={{0,4},{1,5},{2,6},{3,7},{4,0},{5,1},{6,2},{7,3},{8,12},{9,13},{10,... | collective-permute-start | bytes 294920 | tf_op jit(solution)/shard_map/ppermute | solution.py:138
  9.6 33.0 %collective-permute-start.2 = (bf16[24,2048]{1,0:T(8,128)(2,1)S(1)}, bf16[24,2048]{1,0:T(8,128)(2,1)S(1)}, u32[]{:S(2)}, u32[]{:S(2)}) collective-permute-start(bf16[24,2048]{1,0:T(8,128)(2,1)S(1)} %get-tuple-element.12), channel_id=1, source_target_pairs={{0,6},{1,7},{2,4},{3,5},{4,2},{5,3},{6,0},{7,1},{8,14},{9,15},{10,... | collective-permute-start | bytes 294920 | tf_op jit(solution)/shard_map/ppermute | solution.py:138
  10.3 4.3 %collective-permute-start.6 = (bf16[24,1280]{1,0:T(8,128)(2,1)S(1)}, bf16[24,1280]{1,0:T(8,128)(2,1)S(1)}, u32[]{:S(2)}, u32[]{:S(2)}) collective-permute-start(bf16[24,1280]{1,0:T(8,128)(2,1)S(1)} %get-tuple-element.17), channel_id=1, source_target_pairs={{0,24},{1,25},{2,26},{3,27},{4,28},{5,29},{6,30},{7,31},{8,0},{9,1... | collective-permute-start | bytes 184328 | tf_op jit(solution)/shard_map/ppermute | solution.py:148
  11.6 5.1 %collective-permute-start.7 = (bf16[24,1280]{1,0:T(8,128)(2,1)S(1)}, bf16[24,1280]{1,0:T(8,128)(2,1)S(1)}, u32[]{:S(2)}, u32[]{:S(2)}) collective-permute-start(bf16[24,1280]{1,0:T(8,128)(2,1)S(1)} %get-tuple-element.18), channel_id=1, source_target_pairs={{0,25},{1,24},{2,27},{3,26},{4,29},{5,28},{6,31},{7,30},{8,1},{9,0... | collective-permute-start | bytes 184328 | tf_op jit(solution)/shard_map/ppermute | solution.py:148
  14.6 5.8 %collective-permute-start.12 = (bf16[24,1792]{1,0:T(8,128)(2,1)S(1)}, bf16[24,1792]{1,0:T(8,128)(2,1)S(1)}, u32[]{:S(2)}, u32[]{:S(2)}) collective-permute-start(bf16[24,1792]{1,0:T(8,128)(2,1)S(1)} %get-tuple-element.15), channel_id=1, source_target_pairs={{0,24},{1,25},{2,26},{3,27},{4,28},{5,29},{6,30},{7,31},{8,0},{9,1... | collective-permute-start | bytes 258056 | tf_op jit(solution)/shard_map/ppermute | solution.py:148
  16.7 5.2 %collective-permute-start.13 = (bf16[24,1792]{1,0:T(8,128)(2,1)S(1)}, bf16[24,1792]{1,0:T(8,128)(2,1)S(1)}, u32[]{:S(2)}, u32[]{:S(2)}) collective-permute-start(bf16[24,1792]{1,0:T(8,128)(2,1)S(1)} %get-tuple-element.16), channel_id=1, source_target_pairs={{0,25},{1,24},{2,27},{3,26},{4,29},{5,28},{6,31},{7,30},{8,1},{9,0... | collective-permute-start | bytes 258056 | tf_op jit(solution)/shard_map/ppermute | solution.py:148
  20.4 14.6 %collective-permute-start.9 = (bf16[48,1280]{1,0:T(8,128)(2,1)S(1)}, bf16[48,1280]{1,0:T(8,128)(2,1)S(1)}, u32[]{:S(2)}, u32[]{:S(2)}) collective-permute-start(bf16[48,1280]{1,0:T(8,128)(2,1)S(1)} %multiply_convert_fusion.1), channel_id=1, source_target_pairs={{0,4},{1,5},{2,6},{3,7},{4,0},{5,1},{6,2},{7,3},{8,12},{9,13},{10,... | collective-permute-start | bytes 368648 | tf_op jit(solution)/shard_map/ppermute | solution.py:138
  21.9 19.4 %collective-permute-start.8 = (bf16[48,1280]{1,0:T(8,128)(2,1)S(1)}, bf16[48,1280]{1,0:T(8,128)(2,1)S(1)}, u32[]{:S(2)}, u32[]{:S(2)}) collective-permute-start(bf16[48,1280]{1,0:T(8,128)(2,1)S(1)} %multiply_convert_fusion.1), channel_id=1, source_target_pairs={{0,2},{1,3},{2,0},{3,1},{4,6},{5,7},{6,4},{7,5},{8,10},{9,11},{10,... | collective-permute-start | bytes 368648 | tf_op jit(solution)/shard_map/ppermute | solution.py:138
  24.5 10.5 %collective-permute-start.15 = (bf16[48,1792]{1,0:T(8,128)(2,1)S(1)}, bf16[48,1792]{1,0:T(8,128)(2,1)S(1)}, u32[]{:S(2)}, u32[]{:S(2)}) collective-permute-start(bf16[48,1792]{1,0:T(8,128)(2,1)S(1)} %multiply_convert_fusion), channel_id=1, source_target_pairs={{0,4},{1,5},{2,6},{3,7},{4,0},{5,1},{6,2},{7,3},{8,12},{9,13},{10,... | collective-permute-start | bytes 516104 | tf_op jit(solution)/shard_map/ppermute | solution.py:138
  26.1 11.0 %collective-permute-start.14 = (bf16[48,1792]{1,0:T(8,128)(2,1)S(1)}, bf16[48,1792]{1,0:T(8,128)(2,1)S(1)}, u32[]{:S(2)}, u32[]{:S(2)}) collective-permute-start(bf16[48,1792]{1,0:T(8,128)(2,1)S(1)} %multiply_convert_fusion), channel_id=1, source_target_pairs={{0,2},{1,3},{2,0},{3,1},{4,6},{5,7},{6,4},{7,5},{8,10},{9,11},{10,... | collective-permute-start | bytes 516104 | tf_op jit(solution)/shard_map/ppermute | solution.py:138
  35.0 6.2 %collective-permute-start.16 = (bf16[48,1792]{1,0:T(8,128)(2,1)S(1)}, bf16[48,1792]{1,0:T(8,128)(2,1)S(1)}, u32[]{:S(2)}, u32[]{:S(2)}) collective-permute-start(bf16[48,1792]{1,0:T(8,128)(2,1)S(1)} %collective-permute-done.15), channel_id=1, source_target_pairs={{0,2},{1,3},{2,0},{3,1},{4,6},{5,7},{6,4},{7,5},{8,10},{9,11},{10,... | collective-permute-start | bytes 516104 | tf_op jit(solution)/shard_map/ppermute | solution.py:138
  35.0 7.5 %collective-permute-start.10 = (bf16[48,1280]{1,0:T(8,128)(2,1)S(1)}, bf16[48,1280]{1,0:T(8,128)(2,1)S(1)}, u32[]{:S(2)}, u32[]{:S(2)}) collective-permute-start(bf16[48,1280]{1,0:T(8,128)(2,1)S(1)} %collective-permute-done.9), channel_id=1, source_target_pairs={{0,2},{1,3},{2,0},{3,1},{4,6},{5,7},{6,4},{7,5},{8,10},{9,11},{10,... | collective-permute-start | bytes 368648 | tf_op jit(solution)/shard_map/ppermute | solution.py:138
  41.2 5.9 %collective-permute-start.17 = (bf16[192,1792]{1,0:T(8,128)(2,1)S(1)}, bf16[192,1792]{1,0:T(8,128)(2,1)S(1)}, u32[]{:S(2)}, u32[]{:S(2)}) collective-permute-start(bf16[192,1792]{1,0:T(8,128)(2,1)S(1)} %pad_maximum_fusion.rows_ref), channel_id=1, source_target_pairs={{0,1},{1,0},{2,3},{3,2},{4,5},{5,4},{6,7},{7,6},{8,9},{9,8},{10,11... | collective-permute-start | bytes 2064392 | tf_op jit(solution)/shard_map/ppermute | solution.py:135
  42.5 9.1 %collective-permute-start.11 = (bf16[192,1280]{1,0:T(8,128)(2,1)S(1)}, bf16[192,1280]{1,0:T(8,128)(2,1)S(1)}, u32[]{:S(2)}, u32[]{:S(2)}) collective-permute-start(bf16[192,1280]{1,0:T(8,128)(2,1)S(1)} %pad_maximum_fusion.1.rows_ref), channel_id=1, source_target_pairs={{0,1},{1,0},{2,3},{3,2},{4,5},{5,4},{6,7},{7,6},{8,9},{9,8},{10,11... | collective-permute-start | bytes 1474568 | tf_op jit(solution)/shard_map/ppermute | solution.py:135
  42.7 2.1 %collective-permute-start.3 = (bf16[96,1024]{1,0:T(8,128)(2,1)S(1)}, bf16[96,1024]{1,0:T(8,128)(2,1)S(1)}, u32[]{:S(2)}, u32[]{:S(2)}) collective-permute-start(bf16[96,1024]{1,0:T(8,128)(2,1)S(1)} %get-tuple-element.13), channel_id=1, source_target_pairs={{0,1},{1,0},{2,3},{3,2},{4,5},{5,4},{6,7},{7,6},{8,9},{9,8},{10,11... | collective-permute-start | bytes 589832 | tf_op jit(solution)/shard_map/ppermute | solution.py:135

commit v2 on v1

--- a/solution.py
+++ b/solution.py
@@ -7,7 +7,8 @@
 
 
 CORES = 2
-CHUNKS = ((7, True), (5, True))
+CHUNKS = ((5, True), (7, True))
+CALLS = lambda own, rest: ([own[0], rest[0]], [own[1]], [rest[1]])
 TILE = 256
 
 VMEM = pl.BlockSpec(memory_space=pltpu.VMEM)
@@ -53,53 +54,56 @@
 def join_hidden(core, kept, got, chips):
     slots = kept.shape[0] // chips
 
-    def kernel(core_ref, kept_ref, got_ref, out):
+    def kernel(core_ref, kept_ref, got_ref, out, held):
         for k in range(chips):
             own = kept_ref[k * slots : (k + 1) * slots, :]
             other = got_ref[k * slots : (k + 1) * slots, :]
             begin = 2 * k * slots
-            out[begin : begin + slots, :] = jnp.where(core_ref[0] == 0, own, other)
-            out[begin + slots : begin + 2 * slots, :] = jnp.where(core_ref[0] == 0, other, own)
-
+            held[begin : begin + slots, :] = jnp.where(core_ref[0] == 0, own, other)
+            held[begin + slots : begin + 2 * slots, :] = jnp.where(core_ref[0] == 0, other, own)
+        out[...] = held[...].T
+
+    shape = (2 * chips * slots, kept.shape[1])
     return pl.pallas_call(
         kernel,
         in_specs=[SMEM, VMEM, VMEM],
         out_specs=VMEM,
-        out_shape=jax.ShapeDtypeStruct((2 * chips * slots, kept.shape[1]), kept.dtype),
+        out_shape=jax.ShapeDtypeStruct(shape[::-1], kept.dtype),
+        scratch_shapes=[pltpu.VMEM(shape, kept.dtype)],
         compiler_params=pltpu.CompilerParams(vmem_limit_bytes=4 << 20),
         name="join_hidden",
     )(core, kept, got)
 
 
-def product(core, lhs, rows, out, width, half, offset):
-    _, units = lhs.shape
-    size = rows.shape[1]
-    steps = size // TILE
+def product(core, lhs, blocks, out, width):
+    units = lhs.shape[0]
     span = width // 2
-
-    def kernel(core_ref, lhs_ref, rows_ref, *refs):
+    sizes = [rows.shape[1] // TILE for rows, _, _ in blocks]
+
+    def kernel(core_ref, lhs_ref, *refs):
         out_ref, made, sems = refs[-3:]
         mine = core_ref[0]
-        base = (mine if half == 0 else 1 - mine) * span + offset
         copies = []
-        for step in range(steps):
-            made[step] = lax.dot_general(
-                lhs_ref[...],
-                rows_ref[:, step * TILE : (step + 1) * TILE],
-                (((0,), (0,)), ((), ())),
-                preferred_element_type=jnp.float32,
-            ).astype(made.dtype)
-            begin = pl.multiple_of(base + step * TILE, TILE)
-            copy = pltpu.make_async_copy(
-                made.at[step], out_ref.at[:, pl.ds(begin, TILE)], sems.at[step]
-            )
-            copy.start()
-            copies.append(copy)
+        for n, (_, half, offset) in enumerate(blocks):
+            base = (mine if half == 0 else 1 - mine) * span + offset
+            for step in range(sizes[n]):
+                slot = len(copies)
+                made[slot] = jnp.dot(
+                    lhs_ref[...],
+                    refs[n][:, step * TILE : (step + 1) * TILE],
+                    preferred_element_type=jnp.float32,
+                ).astype(made.dtype)
+                begin = pl.multiple_of(base + step * TILE, TILE)
+                copy = pltpu.make_async_copy(
+                    made.at[slot], out_ref.at[:, pl.ds(begin, TILE)], sems.at[slot]
+                )
+                copy.start()
+                copies.append(copy)
         for copy in copies:
             copy.wait()
 
-    operands = [core, lhs, rows]
-    in_specs = [SMEM, VMEM, VMEM]
+    operands = [core, lhs, *(rows for rows, _, _ in blocks)]
+    in_specs = [SMEM] + [VMEM] * (len(operands) - 1)
     aliases = {}
     if out is not None:
         aliases = {len(operands): 0}
@@ -111,11 +115,11 @@
         out_specs=ANY,
         out_shape=jax.ShapeDtypeStruct((units, width), jnp.bfloat16),
         scratch_shapes=[
-            pltpu.VMEM((steps, units, TILE), jnp.bfloat16),
-            pltpu.SemaphoreType.DMA((steps,)),
+            pltpu.VMEM((sum(sizes), units, TILE), jnp.bfloat16),
+            pltpu.SemaphoreType.DMA((sum(sizes),)),
         ],
         input_output_aliases=aliases,
-        compiler_params=pltpu.CompilerParams(vmem_limit_bytes=10 << 20),
+        compiler_params=pltpu.CompilerParams(vmem_limit_bytes=20 << 20),
         name="product",
     )(*operands)
 
@@ -139,6 +143,9 @@
             value, "dp", [(a * CORES + i, b * CORES + i) for a, b in pairs for i in range(CORES)]
         )
 
+    def at(distance, value):
+        return to_chip(value, [(a, a ^ distance) for a in range(chips)])
+
     def back_to(value, flip):
         pairs = [
             (s * members + d, ((s - 1) % sections) * members + (d ^ flip))
@@ -153,9 +160,13 @@
     asked = lax.ppermute(
         slot_token, "pipe", [(s, (s + 1) % sections) for s in range(sections)]
     )
+    factors = live_factors(slot_count, slot_weight[0]).reshape(slots)
+    other_factors = partner(factors)
+    both = in_order(factors, other_factors)[:, None]
+
     hidden_parts = list(split_hidden(place[:1], hidden[0, 0], chips))
     for k in range(1, chips):
-        hidden_parts[k] = to_chip(hidden_parts[k], [(a, a ^ k) for a in range(chips)])
+        hidden_parts[k] = at(k, hidden_parts[k])
     came = jnp.concatenate(hidden_parts)
     units = came.shape[1] // CORES
     low, high = came[:, :units], came[:, units:]
@@ -165,14 +176,8 @@
     positions = lax.broadcasted_iota(jnp.int32, (slots, cotangent.shape[1]), 1)
     chosen = (asked[0, 0][:, None] == positions).astype(jnp.bfloat16)
     rows = jnp.dot(chosen, cotangent[0], preferred_element_type=jnp.bfloat16)
-    factors = live_factors(slot_count, slot_weight[0]).reshape(slots)
-    other_factors = partner(factors)
-    both = in_order(factors, other_factors)[:, None]
-
-    def at(distance, value):
-        return to_chip(value, [(a, a ^ distance) for a in range(chips)])
-
-    out, begin = None, 0
+
+    out, begin, owns, rests = None, 0, [], []
     for share, relayed in CHUNKS:
         end = begin + span * share // sum(part for part, _ in CHUNKS)
         low, high = rows[:, begin:end], rows[:, span + begin : span + end]
@@ -182,14 +187,17 @@
         parts = [pair]
         for k in range(1, chips):
             if relayed and k > 2 and chips == 4:
-                parts.append(at(1, parts[2]))
+                carried = jnp.where(chip < chips, parts[2], pair)
+                parts.append(at(1, carried))
             else:
                 parts.append(at(k, pair))
         whole = jnp.concatenate(parts)
         rest = partner(whole)
-        out = product(place[1:2], lhs, whole, out, width, 0, begin)
-        out = product(place[1:2], lhs, rest, out, width, 1, begin)
+        owns.append((whole, 0, begin))
+        rests.append((rest, 1, begin))
         begin = end
+    for blocks in CALLS(owns, rests):
+        out = product(place[1:2], lhs, blocks, out, width)
     return out[None]
 
 

time: 53.7 us -> 52.6 us (0.980)
  Pallas kernels: 8.9 us -> 7.7 us
    pallas_call x4 -> x3, Pallas kernels: 8.75 us -> 7.41 us  [product(): pl.pallas_call(kernel, in_specs=in_specs, out_specs=ANY, out_shape=jax.Sh...]
  transfers between devices with their start and end apart: 18 -> 18, of which waited for: 6 -> 6; matrix products, arithmetic and copies ran while one was open for 1% -> 2% of each run, Pallas kernels for 13% -> 10%
where the time goes in v2:
time: 52.6 us; the launch traced here: 52.5 us
  starting transfers between devices  20.9 us (40%)
  waiting for transfers between devices  20.5 us (39%)
  Pallas kernels  7.7 us (15%)
  local copies, waits for them, and re-layouts  1.68 us (3%)
  between operations  0.86 us (2%)
    ppermute x9, waiting for transfers between devices, to_chip(): lax.ppermute(value, 'dp', [(a * CORES + i, b * CORES + i) for a, b in pai...  14.1 us
    ppermute x9, starting transfers between devices, to_chip(): lax.ppermute(value, 'dp', [(a * CORES + i, b * CORES + i) for a, b in pai...  12.2 us
    pallas_call x3, Pallas kernels, product(): pl.pallas_call(kernel, in_specs=in_specs, out_specs=ANY, out_shape=jax.Sh...  7.41 us
    ppermute x4, starting transfers between devices, back_to(): return lax.ppermute(value, ('pipe', 'dp'), pairs)  5.06 us
    ppermute x4, waiting for transfers between devices, back_to(): return lax.ppermute(value, ('pipe', 'dp'), pairs)  4.87 us
    ppermute x1, starting transfers between devices, local(): lax.ppermute(slot_token, 'pipe', [(s, (s + 1) % sections) for s in range(...  2.97 us
    unnamed x9, local copies, waits for them, and re-layouts  1.67 us
    ppermute x4, waiting for transfers between devices, partner(): return lax.ppermute(value, 'dp', [(s, s ^ 1) for s in range(members)])  1.52 us
  transfers between devices with their start and end apart: 18, of which 6 were waited for; matrix products, arithmetic and copies ran while one was open for 2% of the time, Pallas kernels for 10%

profile of v2, /device:TPU:0, one launch (start us, length us, event | category | flops | bytes accessed | tf_op | source)
XLA Modules:
  0.0 52.5 jit_solution(14718116575673448642)
XLA Ops:
  0.0 3.0 %collective-permute-start.5 = (s32[1,1,24]{2,1,0:T(1,128)}, s32[1,1,24]{2,1,0:T(1,128)S(1)}, u32[]{:S(2)}, u32[]{:S(2)}) collective-permute-start(s32[1,1,24]{2,1,0:T(1,128)} %param.6), channel_id=1, source_target_pairs={{0,8},{8,16},{16,24},{24,0},{1,9},{9,17},{17,25},{25,1},{2,10},{10... | collective-permute-start | bytes 296 | tf_op jit(solution)/shard_map/ppermute | solution.py:160
  3.6 0.6 %copy-done.2 = f32[1,1,24]{2,1,0:T(1,128)S(1)} copy-done((f32[1,1,24]{2,1,0:T(1,128)S(1)}, f32[1,1,24]{2,1,0:T(1,128)}, u32[]{:S(2)}) %copy-start.2) | copy-done | bytes 120
  4.4 1.0 %copy-done.1 = bf16[1,1,24,8192]{3,2,1,0:T(8,128)(2,1)S(1)} copy-done((bf16[1,1,24,8192]{3,2,1,0:T(8,128)(2,1)S(1)}, bf16[1,1,24,8192]{3,2,1,0:T(8,128)(2,1)}, u32[]{:S(2)}) %copy-start.1) | copy-done | bytes 393240
  5.4 1.6 %collective-permute-start = (bf16[24,2048]{1,0:T(8,128)(2,1)S(1)}, bf16[24,2048]{1,0:T(8,128)(2,1)S(1)}, u32[]{:S(2)}, u32[]{:S(2)}) collective-permute-start(bf16[24,2048]{1,0:T(8,128)(2,1)S(1)} %get-tuple-element.10), channel_id=1, source_target_pairs={{0,2},{1,3},{2,0},{3,1},{4,6},{5,7},{6,4},{7,5},{8,10},{9,11},{10,... | collective-permute-start | bytes 294920 | tf_op jit(solution)/shard_map/ppermute | solution.py:142
  7.0 2.6 %collective-permute-start.1 = (bf16[24,2048]{1,0:T(8,128)(2,1)S(1)}, bf16[24,2048]{1,0:T(8,128)(2,1)S(1)}, u32[]{:S(2)}, u32[]{:S(2)}) collective-permute-start(bf16[24,2048]{1,0:T(8,128)(2,1)S(1)} %get-tuple-element.11), channel_id=1, source_target_pairs={{0,4},{1,5},{2,6},{3,7},{4,0},{5,1},{6,2},{7,3},{8,12},{9,13},{10,... | collective-permute-start | bytes 294920 | tf_op jit(solution)/shard_map/ppermute | solution.py:142
  9.9 0.4 fusion
  10.3 1.3 %collective-permute-start.12 = (bf16[24,1280]{1,0:T(8,128)(2,1)S(1)}, bf16[24,1280]{1,0:T(8,128)(2,1)S(1)}, u32[]{:S(2)}, u32[]{:S(2)}) collective-permute-start(bf16[24,1280]{1,0:T(8,128)(2,1)S(1)} %get-tuple-element.15), channel_id=1, source_target_pairs={{0,24},{1,25},{2,26},{3,27},{4,28},{5,29},{6,30},{7,31},{8,0},{9,1... | collective-permute-start | bytes 184328 | tf_op jit(solution)/shard_map/ppermute | solution.py:155
  11.6 0.8 %collective-permute-start.13 = (bf16[24,1280]{1,0:T(8,128)(2,1)S(1)}, bf16[24,1280]{1,0:T(8,128)(2,1)S(1)}, u32[]{:S(2)}, u32[]{:S(2)}) collective-permute-start(bf16[24,1280]{1,0:T(8,128)(2,1)S(1)} %get-tuple-element.16), channel_id=1, source_target_pairs={{0,25},{1,24},{2,27},{3,26},{4,29},{5,28},{6,31},{7,30},{8,1},{9,0... | collective-permute-start | bytes 184328 | tf_op jit(solution)/shard_map/ppermute | solution.py:155
  12.5 2.1 %collective-permute-done.12 = bf16[24,1280]{1,0:T(8,128)(2,1)S(1)} collective-permute-done((bf16[24,1280]{1,0:T(8,128)(2,1)S(1)}, bf16[24,1280]{1,0:T(8,128)(2,1)S(1)}, u32[]{:S(2)}, u32[]{:S(2)}) %collective-permute-start.12) | collective-permute-done | bytes 61472 | tf_op jit(solution)/shard_map/ppermute | solution.py:155
  14.6 2.1 %collective-permute-start.6 = (bf16[24,1792]{1,0:T(8,128)(2,1)S(1)}, bf16[24,1792]{1,0:T(8,128)(2,1)S(1)}, u32[]{:S(2)}, u32[]{:S(2)}) collective-permute-start(bf16[24,1792]{1,0:T(8,128)(2,1)S(1)} %get-tuple-element.17), channel_id=1, source_target_pairs={{0,24},{1,25},{2,26},{3,27},{4,28},{5,29},{6,30},{7,31},{8,0},{9,1... | collective-permute-start | bytes 258056 | tf_op jit(solution)/shard_map/ppermute | solution.py:155
  16.7 0.8 %collective-permute-start.7 = (bf16[24,1792]{1,0:T(8,128)(2,1)S(1)}, bf16[24,1792]{1,0:T(8,128)(2,1)S(1)}, u32[]{:S(2)}, u32[]{:S(2)}) collective-permute-start(bf16[24,1792]{1,0:T(8,128)(2,1)S(1)} %get-tuple-element.18), channel_id=1, source_target_pairs={{0,25},{1,24},{2,27},{3,26},{4,29},{5,28},{6,31},{7,30},{8,1},{9,0... | collective-permute-start | bytes 258056 | tf_op jit(solution)/shard_map/ppermute | solution.py:155
  17.6 2.8 %collective-permute-done.6 = bf16[24,1792]{1,0:T(8,128)(2,1)S(1)} collective-permute-done((bf16[24,1792]{1,0:T(8,128)(2,1)S(1)}, bf16[24,1792]{1,0:T(8,128)(2,1)S(1)}, u32[]{:S(2)}, u32[]{:S(2)}) %collective-permute-start.6) | collective-permute-done | bytes 86048 | tf_op jit(solution)/shard_map/ppermute | solution.py:155
  20.4 1.5 %collective-permute-start.15 = (bf16[48,1280]{1,0:T(8,128)(2,1)S(1)}, bf16[48,1280]{1,0:T(8,128)(2,1)S(1)}, u32[]{:S(2)}, u32[]{:S(2)}) collective-permute-start(bf16[48,1280]{1,0:T(8,128)(2,1)S(1)} %multiply_convert_fusion.1), channel_id=1, source_target_pairs={{0,4},{1,5},{2,6},{3,7},{4,0},{5,1},{6,2},{7,3},{8,12},{9,13},{10,... | collective-permute-start | bytes 368648 | tf_op jit(solution)/shard_map/ppermute | solution.py:142
  21.9 2.5 %collective-permute-start.14 = (bf16[48,1280]{1,0:T(8,128)(2,1)S(1)}, bf16[48,1280]{1,0:T(8,128)(2,1)S(1)}, u32[]{:S(2)}, u32[]{:S(2)}) collective-permute-start(bf16[48,1280]{1,0:T(8,128)(2,1)S(1)} %multiply_convert_fusion.1), channel_id=1, source_target_pairs={{0,2},{1,3},{2,0},{3,1},{4,6},{5,7},{6,4},{7,5},{8,10},{9,11},{10,... | collective-permute-start | bytes 368648 | tf_op jit(solution)/shard_map/ppermute | solution.py:142
  24.5 1.6 %collective-permute-start.9 = (bf16[48,1792]{1,0:T(8,128)(2,1)S(1)}, bf16[48,1792]{1,0:T(8,128)(2,1)S(1)}, u32[]{:S(2)}, u32[]{:S(2)}) collective-permute-start(bf16[48,1792]{1,0:T(8,128)(2,1)S(1)} %multiply_convert_fusion), channel_id=1, source_target_pairs={{0,4},{1,5},{2,6},{3,7},{4,0},{5,1},{6,2},{7,3},{8,12},{9,13},{10,... | collective-permute-start | bytes 516104 | tf_op jit(solution)/shard_map/ppermute | solution.py:142
  26.2 8.8 %collective-permute-done.9 = bf16[48,1792]{1,0:T(8,128)(2,1)S(1)} collective-permute-done((bf16[48,1792]{1,0:T(8,128)(2,1)S(1)}, bf16[48,1792]{1,0:T(8,128)(2,1)S(1)}, u32[]{:S(2)}, u32[]{:S(2)}) %collective-permute-start.9) | collective-permute-done | bytes 172064 | tf_op jit(solution)/shard_map/ppermute | solution.py:142
  35.1 2.1 %collective-permute-start.16 = (bf16[48,1280]{1,0:T(8,128)(2,1)S(1)}, bf16[48,1280]{1,0:T(8,128)(2,1)S(1)}, u32[]{:S(2)}, u32[]{:S(2)}) collective-permute-start(bf16[48,1280]{1,0:T(8,128)(2,1)S(1)} %broadcast_select_fusion.3), channel_id=1, source_target_pairs={{0,2},{1,3},{2,0},{3,1},{4,6},{5,7},{6,4},{7,5},{8,10},{9,11},{10,... | collective-permute-start | bytes 368648 | tf_op jit(solution)/shard_map/ppermute | solution.py:142
  37.2 4.0 %collective-permute-done.10 = bf16[48,1792]{1,0:T(8,128)(2,1)S(1)} collective-permute-done((bf16[48,1792]{1,0:T(8,128)(2,1)S(1)}, bf16[48,1792]{1,0:T(8,128)(2,1)S(1)}, u32[]{:S(2)}, u32[]{:S(2)}) %collective-permute-start.10) | collective-permute-done | bytes 172064 | tf_op jit(solution)/shard_map/ppermute | solution.py:142
  41.4 1.2 %collective-permute-done.16 = bf16[48,1280]{1,0:T(8,128)(2,1)S(1)} collective-permute-done((bf16[48,1280]{1,0:T(8,128)(2,1)S(1)}, bf16[48,1280]{1,0:T(8,128)(2,1)S(1)}, u32[]{:S(2)}, u32[]{:S(2)}) %collective-permute-start.16) | collective-permute-done | bytes 122912 | tf_op jit(solution)/shard_map/ppermute | solution.py:142
  42.8 0.5 %collective-permute-start.3 = (bf16[96,1024]{1,0:T(8,128)(2,1)S(1)}, bf16[96,1024]{1,0:T(8,128)(2,1)S(1)}, u32[]{:S(2)}, u32[]{:S(2)}) collective-permute-start(bf16[96,1024]{1,0:T(8,128)(2,1)S(1)} %get-tuple-element.13), channel_id=1, source_target_pairs={{0,1},{1,0},{2,3},{3,2},{4,5},{5,4},{6,7},{7,6},{8,9},{9,8},{10,11... | collective-permute-start | bytes 589832 | tf_op jit(solution)/shard_map/ppermute | solution.py:139
  43.3 1.5 %collective-permute-done.3.got_ref = bf16[96,1024]{1,0:T(8,128)(2,1)S(1)} collective-permute-done((bf16[96,1024]{1,0:T(8,128)(2,1)S(1)}, bf16[96,1024]{1,0:T(8,128)(2,1)S(1)}, u32[]{:S(2)}, u32[]{:S(2)}) %collective-permute-start.3) | collective-permute-done | bytes 196640 | tf_op jit(solution)/shard_map/ppermute | solution.py:139
  45.0 2.8 %product.3.refs_1_ = bf16[1024,6144]{1,0:T(8,128)(2,1)} custom-call(s32[1]{0:T(128)} %bitcast.core_ref, bf16[1024,192]{1,0:T(8,128)(2,1)S(1)} %join_hidden.1.lhs_ref, bf16[192,1280]{1,0:T(8,128)(2,1)S(1)} %pad_maximum_fusion.1.refs_0_, bf16[192,1280]{1,0:T(8,128)(2,1)S(1)} %collective-permute-done.17.refs_1_), custom_call_target="tpu_custom_call" | custom-call | tf_op jit(solution)/shard_map/product/pallas_call | solution.py:112
  47.9 2.3 %product.4.refs_1_ = bf16[1024,6144]{1,0:T(8,128)(2,1)} custom-call(s32[1]{0:T(128)} %bitcast.core_ref, bf16[1024,192]{1,0:T(8,128)(2,1)S(1)} %join_hidden.1.lhs_ref, bf16[192,1792]{1,0:T(8,128)(2,1)S(1)} %pad_maximum_fusion.refs_0_, bf16[1024,6144]{1,0:T(8,128)(2,1)} %product.3.refs_1_), custom_call_target="tpu_custom_call", output_to_operand_aliasing={{}: (3, {})} | custom-call | tf_op jit(solution)/shard_map/product/pallas_call | solution.py:112
  50.2 2.3 %product.5 = bf16[1024,6144]{1,0:T(8,128)(2,1)} custom-call(s32[1]{0:T(128)} %bitcast.core_ref, bf16[1024,192]{1,0:T(8,128)(2,1)S(1)} %join_hidden.1.lhs_ref, bf16[192,1792]{1,0:T(8,128)(2,1)S(1)} %collective-permute-done.11.refs_0_, bf16[1024,6144]{1,0:T(8,128)(2,1)} %product.4.refs_1_), custom_call_target="tpu_custom_call", output_to_operand_aliasing={{}: (3, {})} | custom-call | tf_op jit(solution)/shard_map/product/pallas_call | solution.py:112
  (39 shorter events, 1.3 us)
Async XLA Ops:
  0.0 9.9 %copy-start = (bf16[1,128,6144]{2,1,0:T(8,128)(2,1)S(1)}, bf16[1,128,6144]{2,1,0:T(8,128)(2,1)}, u32[]{:S(2)}) copy-start(bf16[1,128,6144]{2,1,0:T(8,128)(2,1)} %param.5) | copy-start | bytes 4718596
  0.0 9.8 %collective-permute-start.5 = (s32[1,1,24]{2,1,0:T(1,128)}, s32[1,1,24]{2,1,0:T(1,128)S(1)}, u32[]{:S(2)}, u32[]{:S(2)}) collective-permute-start(s32[1,1,24]{2,1,0:T(1,128)} %param.6), channel_id=1, source_target_pairs={{0,8},{8,16},{16,24},{24,0},{1,9},{9,17},{17,25},{25,1},{2,10},{10... | collective-permute-start | bytes 296 | tf_op jit(solution)/shard_map/ppermute | solution.py:160
  3.6 0.7 %copy-start.2 = (f32[1,1,24]{2,1,0:T(1,128)S(1)}, f32[1,1,24]{2,1,0:T(1,128)}, u32[]{:S(2)}) copy-start(f32[1,1,24]{2,1,0:T(1,128)} %param.8) | copy-start | bytes 292
  4.4 7.2 %collective-permute-start.4 = (f32[24]{0:T(128)S(1)}, f32[24]{0:T(128)S(1)}, u32[]{:S(2)}, u32[]{:S(2)}) collective-permute-start(f32[24]{0:T(128)S(1)} %bitcast.11), channel_id=1, source_target_pairs={{0,1},{1,0},{2,3},{3,2},{4,5},{5,4},{6,7},{7,6},{8,9},{9,8},{10,11... | collective-permute-start | bytes 296 | tf_op jit(solution)/shard_map/ppermute | solution.py:139
  4.4 1.0 %copy-start.1 = (bf16[1,1,24,8192]{3,2,1,0:T(8,128)(2,1)S(1)}, bf16[1,1,24,8192]{3,2,1,0:T(8,128)(2,1)}, u32[]{:S(2)}) copy-start(bf16[1,1,24,8192]{3,2,1,0:T(8,128)(2,1)} %param.9) | copy-start | bytes 1179652
  5.4 19.1 %collective-permute-start = (bf16[24,2048]{1,0:T(8,128)(2,1)S(1)}, bf16[24,2048]{1,0:T(8,128)(2,1)S(1)}, u32[]{:S(2)}, u32[]{:S(2)}) collective-permute-start(bf16[24,2048]{1,0:T(8,128)(2,1)S(1)} %get-tuple-element.10), channel_id=1, source_target_pairs={{0,2},{1,3},{2,0},{3,1},{4,6},{5,7},{6,4},{7,5},{8,10},{9,11},{10,... | collective-permute-start | bytes 294920 | tf_op jit(solution)/shard_map/ppermute | solution.py:142
  7.0 19.0 %collective-permute-start.1 = (bf16[24,2048]{1,0:T(8,128)(2,1)S(1)}, bf16[24,2048]{1,0:T(8,128)(2,1)S(1)}, u32[]{:S(2)}, u32[]{:S(2)}) collective-permute-start(bf16[24,2048]{1,0:T(8,128)(2,1)S(1)} %get-tuple-element.11), channel_id=1, source_target_pairs={{0,4},{1,5},{2,6},{3,7},{4,0},{5,1},{6,2},{7,3},{8,12},{9,13},{10,... | collective-permute-start | bytes 294920 | tf_op jit(solution)/shard_map/ppermute | solution.py:142
  9.6 33.1 %collective-permute-start.2 = (bf16[24,2048]{1,0:T(8,128)(2,1)S(1)}, bf16[24,2048]{1,0:T(8,128)(2,1)S(1)}, u32[]{:S(2)}, u32[]{:S(2)}) collective-permute-start(bf16[24,2048]{1,0:T(8,128)(2,1)S(1)} %get-tuple-element.12), channel_id=1, source_target_pairs={{0,6},{1,7},{2,4},{3,5},{4,2},{5,3},{6,0},{7,1},{8,14},{9,15},{10,... | collective-permute-start | bytes 294920 | tf_op jit(solution)/shard_map/ppermute | solution.py:142
  10.3 4.3 %collective-permute-start.12 = (bf16[24,1280]{1,0:T(8,128)(2,1)S(1)}, bf16[24,1280]{1,0:T(8,128)(2,1)S(1)}, u32[]{:S(2)}, u32[]{:S(2)}) collective-permute-start(bf16[24,1280]{1,0:T(8,128)(2,1)S(1)} %get-tuple-element.15), channel_id=1, source_target_pairs={{0,24},{1,25},{2,26},{3,27},{4,28},{5,29},{6,30},{7,31},{8,0},{9,1... | collective-permute-start | bytes 184328 | tf_op jit(solution)/shard_map/ppermute | solution.py:155
  11.6 5.1 %collective-permute-start.13 = (bf16[24,1280]{1,0:T(8,128)(2,1)S(1)}, bf16[24,1280]{1,0:T(8,128)(2,1)S(1)}, u32[]{:S(2)}, u32[]{:S(2)}) collective-permute-start(bf16[24,1280]{1,0:T(8,128)(2,1)S(1)} %get-tuple-element.16), channel_id=1, source_target_pairs={{0,25},{1,24},{2,27},{3,26},{4,29},{5,28},{6,31},{7,30},{8,1},{9,0... | collective-permute-start | bytes 184328 | tf_op jit(solution)/shard_map/ppermute | solution.py:155
  14.6 5.8 %collective-permute-start.6 = (bf16[24,1792]{1,0:T(8,128)(2,1)S(1)}, bf16[24,1792]{1,0:T(8,128)(2,1)S(1)}, u32[]{:S(2)}, u32[]{:S(2)}) collective-permute-start(bf16[24,1792]{1,0:T(8,128)(2,1)S(1)} %get-tuple-element.17), channel_id=1, source_target_pairs={{0,24},{1,25},{2,26},{3,27},{4,28},{5,29},{6,30},{7,31},{8,0},{9,1... | collective-permute-start | bytes 258056 | tf_op jit(solution)/shard_map/ppermute | solution.py:155
  16.7 5.2 %collective-permute-start.7 = (bf16[24,1792]{1,0:T(8,128)(2,1)S(1)}, bf16[24,1792]{1,0:T(8,128)(2,1)S(1)}, u32[]{:S(2)}, u32[]{:S(2)}) collective-permute-start(bf16[24,1792]{1,0:T(8,128)(2,1)S(1)} %get-tuple-element.18), channel_id=1, source_target_pairs={{0,25},{1,24},{2,27},{3,26},{4,29},{5,28},{6,31},{7,30},{8,1},{9,0... | collective-permute-start | bytes 258056 | tf_op jit(solution)/shard_map/ppermute | solution.py:155
  20.4 14.7 %collective-permute-start.15 = (bf16[48,1280]{1,0:T(8,128)(2,1)S(1)}, bf16[48,1280]{1,0:T(8,128)(2,1)S(1)}, u32[]{:S(2)}, u32[]{:S(2)}) collective-permute-start(bf16[48,1280]{1,0:T(8,128)(2,1)S(1)} %multiply_convert_fusion.1), channel_id=1, source_target_pairs={{0,4},{1,5},{2,6},{3,7},{4,0},{5,1},{6,2},{7,3},{8,12},{9,13},{10,... | collective-permute-start | bytes 368648 | tf_op jit(solution)/shard_map/ppermute | solution.py:142
  21.9 19.5 %collective-permute-start.14 = (bf16[48,1280]{1,0:T(8,128)(2,1)S(1)}, bf16[48,1280]{1,0:T(8,128)(2,1)S(1)}, u32[]{:S(2)}, u32[]{:S(2)}) collective-permute-start(bf16[48,1280]{1,0:T(8,128)(2,1)S(1)} %multiply_convert_fusion.1), channel_id=1, source_target_pairs={{0,2},{1,3},{2,0},{3,1},{4,6},{5,7},{6,4},{7,5},{8,10},{9,11},{10,... | collective-permute-start | bytes 368648 | tf_op jit(solution)/shard_map/ppermute | solution.py:142
  24.5 10.5 %collective-permute-start.9 = (bf16[48,1792]{1,0:T(8,128)(2,1)S(1)}, bf16[48,1792]{1,0:T(8,128)(2,1)S(1)}, u32[]{:S(2)}, u32[]{:S(2)}) collective-permute-start(bf16[48,1792]{1,0:T(8,128)(2,1)S(1)} %multiply_convert_fusion), channel_id=1, source_target_pairs={{0,4},{1,5},{2,6},{3,7},{4,0},{5,1},{6,2},{7,3},{8,12},{9,13},{10,... | collective-permute-start | bytes 516104 | tf_op jit(solution)/shard_map/ppermute | solution.py:142
  26.1 11.1 %collective-permute-start.8 = (bf16[48,1792]{1,0:T(8,128)(2,1)S(1)}, bf16[48,1792]{1,0:T(8,128)(2,1)S(1)}, u32[]{:S(2)}, u32[]{:S(2)}) collective-permute-start(bf16[48,1792]{1,0:T(8,128)(2,1)S(1)} %multiply_convert_fusion), channel_id=1, source_target_pairs={{0,2},{1,3},{2,0},{3,1},{4,6},{5,7},{6,4},{7,5},{8,10},{9,11},{10,... | collective-permute-start | bytes 516104 | tf_op jit(solution)/shard_map/ppermute | solution.py:142
  35.0 6.2 %collective-permute-start.10 = (bf16[48,1792]{1,0:T(8,128)(2,1)S(1)}, bf16[48,1792]{1,0:T(8,128)(2,1)S(1)}, u32[]{:S(2)}, u32[]{:S(2)}) collective-permute-start(bf16[48,1792]{1,0:T(8,128)(2,1)S(1)} %broadcast_select_fusion.2), channel_id=1, source_target_pairs={{0,2},{1,3},{2,0},{3,1},{4,6},{5,7},{6,4},{7,5},{8,10},{9,11},{10,... | collective-permute-start | bytes 516104 | tf_op jit(solution)/shard_map/ppermute | solution.py:142
  35.1 7.4 %collective-permute-start.16 = (bf16[48,1280]{1,0:T(8,128)(2,1)S(1)}, bf16[48,1280]{1,0:T(8,128)(2,1)S(1)}, u32[]{:S(2)}, u32[]{:S(2)}) collective-permute-start(bf16[48,1280]{1,0:T(8,128)(2,1)S(1)} %broadcast_select_fusion.3), channel_id=1, source_target_pairs={{0,2},{1,3},{2,0},{3,1},{4,6},{5,7},{6,4},{7,5},{8,10},{9,11},{10,... | collective-permute-start | bytes 368648 | tf_op jit(solution)/shard_map/ppermute | solution.py:142
  41.3 8.9 %collective-permute-start.11 = (bf16[192,1792]{1,0:T(8,128)(2,1)S(1)}, bf16[192,1792]{1,0:T(8,128)(2,1)S(1)}, u32[]{:S(2)}, u32[]{:S(2)}) collective-permute-start(bf16[192,1792]{1,0:T(8,128)(2,1)S(1)} %pad_maximum_fusion.refs_0_), channel_id=1, source_target_pairs={{0,1},{1,0},{2,3},{3,2},{4,5},{5,4},{6,7},{7,6},{8,9},{9,8},{10,11... | collective-permute-start | bytes 2064392 | tf_op jit(solution)/shard_map/ppermute | solution.py:139
  42.6 2.4 %collective-permute-start.17 = (bf16[192,1280]{1,0:T(8,128)(2,1)S(1)}, bf16[192,1280]{1,0:T(8,128)(2,1)S(1)}, u32[]{:S(2)}, u32[]{:S(2)}) collective-permute-start(bf16[192,1280]{1,0:T(8,128)(2,1)S(1)} %pad_maximum_fusion.1.refs_0_), channel_id=1, source_target_pairs={{0,1},{1,0},{2,3},{3,2},{4,5},{5,4},{6,7},{7,6},{8,9},{9,8},{10,11... | collective-permute-start | bytes 1474568 | tf_op jit(solution)/shard_map/ppermute | solution.py:139
  42.8 2.1 %collective-permute-start.3 = (bf16[96,1024]{1,0:T(8,128)(2,1)S(1)}, bf16[96,1024]{1,0:T(8,128)(2,1)S(1)}, u32[]{:S(2)}, u32[]{:S(2)}) collective-permute-start(bf16[96,1024]{1,0:T(8,128)(2,1)S(1)} %get-tuple-element.13), channel_id=1, source_target_pairs={{0,1},{1,0},{2,3},{3,2},{4,5},{5,4},{6,7},{7,6},{8,9},{9,8},{10,11... | collective-permute-start | bytes 589832 | tf_op jit(solution)/shard_map/ppermute | solution.py:139

commit v3 on v2

--- a/solution.py
+++ b/solution.py
@@ -7,8 +7,8 @@
 
 
 CORES = 2
-CHUNKS = ((5, True), (7, True))
-CALLS = lambda own, rest: ([own[0], rest[0]], [own[1]], [rest[1]])
+CHUNKS = ((11, True), (13, True))
+CALLS = lambda own, rest: ([own[0]], [rest[0]], [own[1]], [rest[1]])
 TILE = 256
 
 VMEM = pl.BlockSpec(memory_space=pltpu.VMEM)
@@ -78,27 +78,31 @@
 def product(core, lhs, blocks, out, width):
     units = lhs.shape[0]
     span = width // 2
-    sizes = [rows.shape[1] // TILE for rows, _, _ in blocks]
+    steps = [
+        (n, half, offset, at, min(TILE, rows.shape[1] - at))
+        for n, (rows, half, offset) in enumerate(blocks)
+        for at in range(0, rows.shape[1], TILE)
+    ]
 
     def kernel(core_ref, lhs_ref, *refs):
         out_ref, made, sems = refs[-3:]
         mine = core_ref[0]
         copies = []
-        for n, (_, half, offset) in enumerate(blocks):
-            base = (mine if half == 0 else 1 - mine) * span + offset
-            for step in range(sizes[n]):
-                slot = len(copies)
-                made[slot] = jnp.dot(
-                    lhs_ref[...],
-                    refs[n][:, step * TILE : (step + 1) * TILE],
-                    preferred_element_type=jnp.float32,
-                ).astype(made.dtype)
-                begin = pl.multiple_of(base + step * TILE, TILE)
-                copy = pltpu.make_async_copy(
-                    made.at[slot], out_ref.at[:, pl.ds(begin, TILE)], sems.at[slot]
+        for slot, (n, half, offset, at, size) in enumerate(steps):
+            made[slot, :, :size] = jnp.dot(
+                lhs_ref[...],
+                refs[n][:, at : at + size],
+                preferred_element_type=jnp.float32,
+            ).astype(made.dtype)
+            begin = (mine if half == 0 else 1 - mine) * span + offset + at
+            copies.append(
+                pltpu.make_async_copy(
+                    made.at[slot, :, pl.ds(0, size)],
+                    out_ref.at[:, pl.ds(pl.multiple_of(begin, 128), size)],
+                    sems.at[slot],
                 )
-                copy.start()
-                copies.append(copy)
+            )
+            copies[-1].start()
         for copy in copies:
             copy.wait()
 
@@ -115,8 +119,8 @@
         out_specs=ANY,
         out_shape=jax.ShapeDtypeStruct((units, width), jnp.bfloat16),
         scratch_shapes=[
-            pltpu.VMEM((sum(sizes), units, TILE), jnp.bfloat16),
-            pltpu.SemaphoreType.DMA((sum(sizes),)),
+            pltpu.VMEM((len(steps), units, TILE), jnp.bfloat16),
+            pltpu.SemaphoreType.DMA((len(steps),)),
         ],
         input_output_aliases=aliases,
         compiler_params=pltpu.CompilerParams(vmem_limit_bytes=20 << 20),

time: 52.6 us -> 53.4 us (1.015)
  Pallas kernels: 7.7 us -> 8.78 us
  waiting for transfers between devices: 20.5 us -> 19.7 us
    pallas_call x3 -> x4, Pallas kernels: 7.41 us -> 8.49 us  [product(): pl.pallas_call(kernel, in_specs=in_specs, out_specs=ANY, out_shape=jax.Sh...]
    ppermute x9, waiting for transfers between devices: 14.1 us -> 13.1 us  [to_chip(): lax.ppermute(value, 'dp', [(a * CORES + i, b * CORES + i) for a, b in pai...]
  transfers between devices with their start and end apart: 18 -> 18, of which waited for: 6 -> 7; matrix products, arithmetic and copies ran while one was open for 2% -> 2% of each run, Pallas kernels for 10% -> 12%
where the time goes in v3:
time: 53.4 us; the launch traced here: 53.2 us
  starting transfers between devices  21.3 us (40%)
  waiting for transfers between devices  19.7 us (37%)
  Pallas kernels  8.78 us (16%)
  local copies, waits for them, and re-layouts  1.68 us (3%)
  between operations  0.87 us (2%)
    ppermute x9, waiting for transfers between devices, to_chip(): lax.ppermute(value, 'dp', [(a * CORES + i, b * CORES + i) for a, b in pai...  13.1 us
    ppermute x9, starting transfers between devices, to_chip(): lax.ppermute(value, 'dp', [(a * CORES + i, b * CORES + i) for a, b in pai...  12.6 us
    pallas_call x4, Pallas kernels, product(): pl.pallas_call(kernel, in_specs=in_specs, out_specs=ANY, out_shape=jax.Sh...  8.49 us
    ppermute x4, starting transfers between devices, back_to(): return lax.ppermute(value, ('pipe', 'dp'), pairs)  5.06 us
    ppermute x4, waiting for transfers between devices, back_to(): return lax.ppermute(value, ('pipe', 'dp'), pairs)  4.93 us
    ppermute x1, starting transfers between devices, local(): lax.ppermute(slot_token, 'pipe', [(s, (s + 1) % sections) for s in range(...  2.97 us
    ppermute x4, waiting for transfers between devices, partner(): return lax.ppermute(value, 'dp', [(s, s ^ 1) for s in range(members)])  1.73 us
    unnamed x9, local copies, waits for them, and re-layouts  1.67 us
  transfers between devices with their start and end apart: 18, of which 7 were waited for; matrix products, arithmetic and copies ran while one was open for 2% of the time, Pallas kernels for 12%

profile of v3, /device:TPU:0, one launch (start us, length us, event | category | flops | bytes accessed | tf_op | source)
XLA Modules:
  0.0 53.2 jit_solution(16525810281984426599)
XLA Ops:
  0.0 3.0 %collective-permute-start.5 = (s32[1,1,24]{2,1,0:T(1,128)}, s32[1,1,24]{2,1,0:T(1,128)S(1)}, u32[]{:S(2)}, u32[]{:S(2)}) collective-permute-start(s32[1,1,24]{2,1,0:T(1,128)} %param.6), channel_id=1, source_target_pairs={{0,8},{8,16},{16,24},{24,0},{1,9},{9,17},{17,25},{25,1},{2,10},{10... | collective-permute-start | bytes 296 | tf_op jit(solution)/shard_map/ppermute | solution.py:164
  3.6 0.6 %copy-done.2 = f32[1,1,24]{2,1,0:T(1,128)S(1)} copy-done((f32[1,1,24]{2,1,0:T(1,128)S(1)}, f32[1,1,24]{2,1,0:T(1,128)}, u32[]{:S(2)}) %copy-start.2) | copy-done | bytes 120
  4.4 1.0 %copy-done.1 = bf16[1,1,24,8192]{3,2,1,0:T(8,128)(2,1)S(1)} copy-done((bf16[1,1,24,8192]{3,2,1,0:T(8,128)(2,1)S(1)}, bf16[1,1,24,8192]{3,2,1,0:T(8,128)(2,1)}, u32[]{:S(2)}) %copy-start.1) | copy-done | bytes 393240
  5.4 1.6 %collective-permute-start = (bf16[24,2048]{1,0:T(8,128)(2,1)S(1)}, bf16[24,2048]{1,0:T(8,128)(2,1)S(1)}, u32[]{:S(2)}, u32[]{:S(2)}) collective-permute-start(bf16[24,2048]{1,0:T(8,128)(2,1)S(1)} %get-tuple-element.10), channel_id=1, source_target_pairs={{0,2},{1,3},{2,0},{3,1},{4,6},{5,7},{6,4},{7,5},{8,10},{9,11},{10,... | collective-permute-start | bytes 294920 | tf_op jit(solution)/shard_map/ppermute | solution.py:146
  7.0 2.6 %collective-permute-start.1 = (bf16[24,2048]{1,0:T(8,128)(2,1)S(1)}, bf16[24,2048]{1,0:T(8,128)(2,1)S(1)}, u32[]{:S(2)}, u32[]{:S(2)}) collective-permute-start(bf16[24,2048]{1,0:T(8,128)(2,1)S(1)} %get-tuple-element.11), channel_id=1, source_target_pairs={{0,4},{1,5},{2,6},{3,7},{4,0},{5,1},{6,2},{7,3},{8,12},{9,13},{10,... | collective-permute-start | bytes 294920 | tf_op jit(solution)/shard_map/ppermute | solution.py:146
  10.3 1.3 %collective-permute-start.12 = (bf16[24,1408]{1,0:T(8,128)(2,1)S(1)}, bf16[24,1408]{1,0:T(8,128)(2,1)S(1)}, u32[]{:S(2)}, u32[]{:S(2)}) collective-permute-start(bf16[24,1408]{1,0:T(8,128)(2,1)S(1)} %get-tuple-element.15), channel_id=1, source_target_pairs={{0,24},{1,25},{2,26},{3,27},{4,28},{5,29},{6,30},{7,31},{8,0},{9,1... | collective-permute-start | bytes 202760 | tf_op jit(solution)/shard_map/ppermute | solution.py:159
  11.6 0.8 %collective-permute-start.13 = (bf16[24,1408]{1,0:T(8,128)(2,1)S(1)}, bf16[24,1408]{1,0:T(8,128)(2,1)S(1)}, u32[]{:S(2)}, u32[]{:S(2)}) collective-permute-start(bf16[24,1408]{1,0:T(8,128)(2,1)S(1)} %get-tuple-element.16), channel_id=1, source_target_pairs={{0,25},{1,24},{2,27},{3,26},{4,29},{5,28},{6,31},{7,30},{8,1},{9,0... | collective-permute-start | bytes 202760 | tf_op jit(solution)/shard_map/ppermute | solution.py:159
  12.5 2.2 %collective-permute-done.12 = bf16[24,1408]{1,0:T(8,128)(2,1)S(1)} collective-permute-done((bf16[24,1408]{1,0:T(8,128)(2,1)S(1)}, bf16[24,1408]{1,0:T(8,128)(2,1)S(1)}, u32[]{:S(2)}, u32[]{:S(2)}) %collective-permute-start.12) | collective-permute-done | bytes 67616 | tf_op jit(solution)/shard_map/ppermute | solution.py:159
  14.7 2.1 %collective-permute-start.6 = (bf16[24,1664]{1,0:T(8,128)(2,1)S(1)}, bf16[24,1664]{1,0:T(8,128)(2,1)S(1)}, u32[]{:S(2)}, u32[]{:S(2)}) collective-permute-start(bf16[24,1664]{1,0:T(8,128)(2,1)S(1)} %get-tuple-element.17), channel_id=1, source_target_pairs={{0,24},{1,25},{2,26},{3,27},{4,28},{5,29},{6,30},{7,31},{8,0},{9,1... | collective-permute-start | bytes 239624 | tf_op jit(solution)/shard_map/ppermute | solution.py:159
  16.8 0.9 %collective-permute-start.7 = (bf16[24,1664]{1,0:T(8,128)(2,1)S(1)}, bf16[24,1664]{1,0:T(8,128)(2,1)S(1)}, u32[]{:S(2)}, u32[]{:S(2)}) collective-permute-start(bf16[24,1664]{1,0:T(8,128)(2,1)S(1)} %get-tuple-element.18), channel_id=1, source_target_pairs={{0,25},{1,24},{2,27},{3,26},{4,29},{5,28},{6,31},{7,30},{8,1},{9,0... | collective-permute-start | bytes 239624 | tf_op jit(solution)/shard_map/ppermute | solution.py:159
  17.7 2.7 %collective-permute-done.6 = bf16[24,1664]{1,0:T(8,128)(2,1)S(1)} collective-permute-done((bf16[24,1664]{1,0:T(8,128)(2,1)S(1)}, bf16[24,1664]{1,0:T(8,128)(2,1)S(1)}, u32[]{:S(2)}, u32[]{:S(2)}) %collective-permute-start.6) | collective-permute-done | bytes 79904 | tf_op jit(solution)/shard_map/ppermute | solution.py:159
  20.5 1.5 %collective-permute-start.15 = (bf16[48,1408]{1,0:T(8,128)(2,1)S(1)}, bf16[48,1408]{1,0:T(8,128)(2,1)S(1)}, u32[]{:S(2)}, u32[]{:S(2)}) collective-permute-start(bf16[48,1408]{1,0:T(8,128)(2,1)S(1)} %multiply_convert_fusion.1), channel_id=1, source_target_pairs={{0,4},{1,5},{2,6},{3,7},{4,0},{5,1},{6,2},{7,3},{8,12},{9,13},{10,... | collective-permute-start | bytes 405512 | tf_op jit(solution)/shard_map/ppermute | solution.py:146
  21.9 2.5 %collective-permute-start.14 = (bf16[48,1408]{1,0:T(8,128)(2,1)S(1)}, bf16[48,1408]{1,0:T(8,128)(2,1)S(1)}, u32[]{:S(2)}, u32[]{:S(2)}) collective-permute-start(bf16[48,1408]{1,0:T(8,128)(2,1)S(1)} %multiply_convert_fusion.1), channel_id=1, source_target_pairs={{0,2},{1,3},{2,0},{3,1},{4,6},{5,7},{6,4},{7,5},{8,10},{9,11},{10,... | collective-permute-start | bytes 405512 | tf_op jit(solution)/shard_map/ppermute | solution.py:146
  24.5 1.5 %collective-permute-start.9 = (bf16[48,1664]{1,0:T(8,128)(2,1)S(1)}, bf16[48,1664]{1,0:T(8,128)(2,1)S(1)}, u32[]{:S(2)}, u32[]{:S(2)}) collective-permute-start(bf16[48,1664]{1,0:T(8,128)(2,1)S(1)} %multiply_convert_fusion), channel_id=1, source_target_pairs={{0,4},{1,5},{2,6},{3,7},{4,0},{5,1},{6,2},{7,3},{8,12},{9,13},{10,... | collective-permute-start | bytes 479240 | tf_op jit(solution)/shard_map/ppermute | solution.py:146
  26.1 2.7 %collective-permute-done.15 = bf16[48,1408]{1,0:T(8,128)(2,1)S(1)} collective-permute-done((bf16[48,1408]{1,0:T(8,128)(2,1)S(1)}, bf16[48,1408]{1,0:T(8,128)(2,1)S(1)}, u32[]{:S(2)}, u32[]{:S(2)}) %collective-permute-start.15) | collective-permute-done | bytes 135200 | tf_op jit(solution)/shard_map/ppermute | solution.py:146
  28.8 2.6 %collective-permute-start.16 = (bf16[48,1408]{1,0:T(8,128)(2,1)S(1)}, bf16[48,1408]{1,0:T(8,128)(2,1)S(1)}, u32[]{:S(2)}, u32[]{:S(2)}) collective-permute-start(bf16[48,1408]{1,0:T(8,128)(2,1)S(1)} %broadcast_select_fusion.3), channel_id=1, source_target_pairs={{0,2},{1,3},{2,0},{3,1},{4,6},{5,7},{6,4},{7,5},{8,10},{9,11},{10,... | collective-permute-start | bytes 405512 | tf_op jit(solution)/shard_map/ppermute | solution.py:146
  31.4 3.5 %collective-permute-done.9 = bf16[48,1664]{1,0:T(8,128)(2,1)S(1)} collective-permute-done((bf16[48,1664]{1,0:T(8,128)(2,1)S(1)}, bf16[48,1664]{1,0:T(8,128)(2,1)S(1)}, u32[]{:S(2)}, u32[]{:S(2)}) %collective-permute-start.9) | collective-permute-done | bytes 159776 | tf_op jit(solution)/shard_map/ppermute | solution.py:146
  35.0 4.5 %collective-permute-done.16 = bf16[48,1408]{1,0:T(8,128)(2,1)S(1)} collective-permute-done((bf16[48,1408]{1,0:T(8,128)(2,1)S(1)}, bf16[48,1408]{1,0:T(8,128)(2,1)S(1)}, u32[]{:S(2)}, u32[]{:S(2)}) %collective-permute-start.16) | collective-permute-done | bytes 135200 | tf_op jit(solution)/shard_map/ppermute | solution.py:146
  39.6 2.4 %collective-permute-done.10 = bf16[48,1664]{1,0:T(8,128)(2,1)S(1)} collective-permute-done((bf16[48,1664]{1,0:T(8,128)(2,1)S(1)}, bf16[48,1664]{1,0:T(8,128)(2,1)S(1)}, u32[]{:S(2)}, u32[]{:S(2)}) %collective-permute-start.10) | collective-permute-done | bytes 159776 | tf_op jit(solution)/shard_map/ppermute | solution.py:146
  42.8 1.7 %collective-permute-done.3.got_ref = bf16[96,1024]{1,0:T(8,128)(2,1)S(1)} collective-permute-done((bf16[96,1024]{1,0:T(8,128)(2,1)S(1)}, bf16[96,1024]{1,0:T(8,128)(2,1)S(1)}, u32[]{:S(2)}, u32[]{:S(2)}) %collective-permute-start.3) | collective-permute-done | bytes 196640 | tf_op jit(solution)/shard_map/ppermute | solution.py:143
  44.7 2.0 %product.4.refs_1_ = bf16[1024,6144]{1,0:T(8,128)(2,1)} custom-call(s32[1]{0:T(128)} %bitcast.core_ref, bf16[1024,192]{1,0:T(8,128)(2,1)S(1)} %join_hidden.1.lhs_ref, bf16[192,1408]{1,0:T(8,128)(2,1)S(1)} %pad_maximum_fusion.1.refs_0_), custom_call_target="tpu_custom_call" | custom-call | tf_op jit(solution)/shard_map/product/pallas_call | solution.py:116
  46.8 2.0 %product.5.refs_1_ = bf16[1024,6144]{1,0:T(8,128)(2,1)} custom-call(s32[1]{0:T(128)} %bitcast.core_ref, bf16[1024,192]{1,0:T(8,128)(2,1)S(1)} %join_hidden.1.lhs_ref, bf16[192,1408]{1,0:T(8,128)(2,1)S(1)} %collective-permute-done.17.refs_0_, bf16[1024,6144]{1,0:T(8,128)(2,1)} %product.4.refs_1_), custom_call_target="tpu_custom_call", output_to_operand_aliasing={{}: (3, {})} | custom-call | tf_op jit(solution)/shard_map/product/pallas_call | solution.py:116
  48.8 2.2 %product.6.refs_1_ = bf16[1024,6144]{1,0:T(8,128)(2,1)} custom-call(s32[1]{0:T(128)} %bitcast.core_ref, bf16[1024,192]{1,0:T(8,128)(2,1)S(1)} %join_hidden.1.lhs_ref, bf16[192,1664]{1,0:T(8,128)(2,1)S(1)} %pad_maximum_fusion.refs_0_, bf16[1024,6144]{1,0:T(8,128)(2,1)} %product.5.refs_1_), custom_call_target="tpu_custom_call", output_to_operand_aliasing={{}: (3, {})} | custom-call | tf_op jit(solution)/shard_map/product/pallas_call | solution.py:116
  51.0 2.2 %product.7 = bf16[1024,6144]{1,0:T(8,128)(2,1)} custom-call(s32[1]{0:T(128)} %bitcast.core_ref, bf16[1024,192]{1,0:T(8,128)(2,1)S(1)} %join_hidden.1.lhs_ref, bf16[192,1664]{1,0:T(8,128)(2,1)S(1)} %collective-permute-done.11.refs_0_, bf16[1024,6144]{1,0:T(8,128)(2,1)} %product.6.refs_1_), custom_call_target="tpu_custom_call", output_to_operand_aliasing={{}: (3, {})} | custom-call | tf_op jit(solution)/shard_map/product/pallas_call | solution.py:116
  (40 shorter events, 2.2 us)
Async XLA Ops:
  0.0 9.9 %copy-start = (bf16[1,128,6144]{2,1,0:T(8,128)(2,1)S(1)}, bf16[1,128,6144]{2,1,0:T(8,128)(2,1)}, u32[]{:S(2)}) copy-start(bf16[1,128,6144]{2,1,0:T(8,128)(2,1)} %param.5) | copy-start | bytes 4718596
  0.0 9.8 %collective-permute-start.5 = (s32[1,1,24]{2,1,0:T(1,128)}, s32[1,1,24]{2,1,0:T(1,128)S(1)}, u32[]{:S(2)}, u32[]{:S(2)}) collective-permute-start(s32[1,1,24]{2,1,0:T(1,128)} %param.6), channel_id=1, source_target_pairs={{0,8},{8,16},{16,24},{24,0},{1,9},{9,17},{17,25},{25,1},{2,10},{10... | collective-permute-start | bytes 296 | tf_op jit(solution)/shard_map/ppermute | solution.py:164
  3.6 0.7 %copy-start.2 = (f32[1,1,24]{2,1,0:T(1,128)S(1)}, f32[1,1,24]{2,1,0:T(1,128)}, u32[]{:S(2)}) copy-start(f32[1,1,24]{2,1,0:T(1,128)} %param.8) | copy-start | bytes 292
  4.4 7.2 %collective-permute-start.4 = (f32[24]{0:T(128)S(1)}, f32[24]{0:T(128)S(1)}, u32[]{:S(2)}, u32[]{:S(2)}) collective-permute-start(f32[24]{0:T(128)S(1)} %bitcast.11), channel_id=1, source_target_pairs={{0,1},{1,0},{2,3},{3,2},{4,5},{5,4},{6,7},{7,6},{8,9},{9,8},{10,11... | collective-permute-start | bytes 296 | tf_op jit(solution)/shard_map/ppermute | solution.py:143
  4.4 1.0 %copy-start.1 = (bf16[1,1,24,8192]{3,2,1,0:T(8,128)(2,1)S(1)}, bf16[1,1,24,8192]{3,2,1,0:T(8,128)(2,1)}, u32[]{:S(2)}) copy-start(bf16[1,1,24,8192]{3,2,1,0:T(8,128)(2,1)} %param.9) | copy-start | bytes 1179652
  5.4 19.1 %collective-permute-start = (bf16[24,2048]{1,0:T(8,128)(2,1)S(1)}, bf16[24,2048]{1,0:T(8,128)(2,1)S(1)}, u32[]{:S(2)}, u32[]{:S(2)}) collective-permute-start(bf16[24,2048]{1,0:T(8,128)(2,1)S(1)} %get-tuple-element.10), channel_id=1, source_target_pairs={{0,2},{1,3},{2,0},{3,1},{4,6},{5,7},{6,4},{7,5},{8,10},{9,11},{10,... | collective-permute-start | bytes 294920 | tf_op jit(solution)/shard_map/ppermute | solution.py:146
  7.0 19.0 %collective-permute-start.1 = (bf16[24,2048]{1,0:T(8,128)(2,1)S(1)}, bf16[24,2048]{1,0:T(8,128)(2,1)S(1)}, u32[]{:S(2)}, u32[]{:S(2)}) collective-permute-start(bf16[24,2048]{1,0:T(8,128)(2,1)S(1)} %get-tuple-element.11), channel_id=1, source_target_pairs={{0,4},{1,5},{2,6},{3,7},{4,0},{5,1},{6,2},{7,3},{8,12},{9,13},{10,... | collective-permute-start | bytes 294920 | tf_op jit(solution)/shard_map/ppermute | solution.py:146
  9.6 32.5 %collective-permute-start.2 = (bf16[24,2048]{1,0:T(8,128)(2,1)S(1)}, bf16[24,2048]{1,0:T(8,128)(2,1)S(1)}, u32[]{:S(2)}, u32[]{:S(2)}) collective-permute-start(bf16[24,2048]{1,0:T(8,128)(2,1)S(1)} %get-tuple-element.12), channel_id=1, source_target_pairs={{0,6},{1,7},{2,4},{3,5},{4,2},{5,3},{6,0},{7,1},{8,14},{9,15},{10,... | collective-permute-start | bytes 294920 | tf_op jit(solution)/shard_map/ppermute | solution.py:146
  10.3 4.4 %collective-permute-start.12 = (bf16[24,1408]{1,0:T(8,128)(2,1)S(1)}, bf16[24,1408]{1,0:T(8,128)(2,1)S(1)}, u32[]{:S(2)}, u32[]{:S(2)}) collective-permute-start(bf16[24,1408]{1,0:T(8,128)(2,1)S(1)} %get-tuple-element.15), channel_id=1, source_target_pairs={{0,24},{1,25},{2,26},{3,27},{4,28},{5,29},{6,30},{7,31},{8,0},{9,1... | collective-permute-start | bytes 202760 | tf_op jit(solution)/shard_map/ppermute | solution.py:159
  11.6 5.2 %collective-permute-start.13 = (bf16[24,1408]{1,0:T(8,128)(2,1)S(1)}, bf16[24,1408]{1,0:T(8,128)(2,1)S(1)}, u32[]{:S(2)}, u32[]{:S(2)}) collective-permute-start(bf16[24,1408]{1,0:T(8,128)(2,1)S(1)} %get-tuple-element.16), channel_id=1, source_target_pairs={{0,25},{1,24},{2,27},{3,26},{4,29},{5,28},{6,31},{7,30},{8,1},{9,0... | collective-permute-start | bytes 202760 | tf_op jit(solution)/shard_map/ppermute | solution.py:159
  14.7 5.8 %collective-permute-start.6 = (bf16[24,1664]{1,0:T(8,128)(2,1)S(1)}, bf16[24,1664]{1,0:T(8,128)(2,1)S(1)}, u32[]{:S(2)}, u32[]{:S(2)}) collective-permute-start(bf16[24,1664]{1,0:T(8,128)(2,1)S(1)} %get-tuple-element.17), channel_id=1, source_target_pairs={{0,24},{1,25},{2,26},{3,27},{4,28},{5,29},{6,30},{7,31},{8,0},{9,1... | collective-permute-start | bytes 239624 | tf_op jit(solution)/shard_map/ppermute | solution.py:159
  16.8 5.2 %collective-permute-start.7 = (bf16[24,1664]{1,0:T(8,128)(2,1)S(1)}, bf16[24,1664]{1,0:T(8,128)(2,1)S(1)}, u32[]{:S(2)}, u32[]{:S(2)}) collective-permute-start(bf16[24,1664]{1,0:T(8,128)(2,1)S(1)} %get-tuple-element.18), channel_id=1, source_target_pairs={{0,25},{1,24},{2,27},{3,26},{4,29},{5,28},{6,31},{7,30},{8,1},{9,0... | collective-permute-start | bytes 239624 | tf_op jit(solution)/shard_map/ppermute | solution.py:159
  20.5 8.3 %collective-permute-start.15 = (bf16[48,1408]{1,0:T(8,128)(2,1)S(1)}, bf16[48,1408]{1,0:T(8,128)(2,1)S(1)}, u32[]{:S(2)}, u32[]{:S(2)}) collective-permute-start(bf16[48,1408]{1,0:T(8,128)(2,1)S(1)} %multiply_convert_fusion.1), channel_id=1, source_target_pairs={{0,4},{1,5},{2,6},{3,7},{4,0},{5,1},{6,2},{7,3},{8,12},{9,13},{10,... | collective-permute-start | bytes 405512 | tf_op jit(solution)/shard_map/ppermute | solution.py:146
  21.9 13.0 %collective-permute-start.14 = (bf16[48,1408]{1,0:T(8,128)(2,1)S(1)}, bf16[48,1408]{1,0:T(8,128)(2,1)S(1)}, u32[]{:S(2)}, u32[]{:S(2)}) collective-permute-start(bf16[48,1408]{1,0:T(8,128)(2,1)S(1)} %multiply_convert_fusion.1), channel_id=1, source_target_pairs={{0,2},{1,3},{2,0},{3,1},{4,6},{5,7},{6,4},{7,5},{8,10},{9,11},{10,... | collective-permute-start | bytes 405512 | tf_op jit(solution)/shard_map/ppermute | solution.py:146
  24.5 10.3 %collective-permute-start.9 = (bf16[48,1664]{1,0:T(8,128)(2,1)S(1)}, bf16[48,1664]{1,0:T(8,128)(2,1)S(1)}, u32[]{:S(2)}, u32[]{:S(2)}) collective-permute-start(bf16[48,1664]{1,0:T(8,128)(2,1)S(1)} %multiply_convert_fusion), channel_id=1, source_target_pairs={{0,4},{1,5},{2,6},{3,7},{4,0},{5,1},{6,2},{7,3},{8,12},{9,13},{10,... | collective-permute-start | bytes 479240 | tf_op jit(solution)/shard_map/ppermute | solution.py:146
  26.0 13.6 %collective-permute-start.8 = (bf16[48,1664]{1,0:T(8,128)(2,1)S(1)}, bf16[48,1664]{1,0:T(8,128)(2,1)S(1)}, u32[]{:S(2)}, u32[]{:S(2)}) collective-permute-start(bf16[48,1664]{1,0:T(8,128)(2,1)S(1)} %multiply_convert_fusion), channel_id=1, source_target_pairs={{0,2},{1,3},{2,0},{3,1},{4,6},{5,7},{6,4},{7,5},{8,10},{9,11},{10,... | collective-permute-start | bytes 479240 | tf_op jit(solution)/shard_map/ppermute | solution.py:146
  28.8 10.7 %collective-permute-start.16 = (bf16[48,1408]{1,0:T(8,128)(2,1)S(1)}, bf16[48,1408]{1,0:T(8,128)(2,1)S(1)}, u32[]{:S(2)}, u32[]{:S(2)}) collective-permute-start(bf16[48,1408]{1,0:T(8,128)(2,1)S(1)} %broadcast_select_fusion.3), channel_id=1, source_target_pairs={{0,2},{1,3},{2,0},{3,1},{4,6},{5,7},{6,4},{7,5},{8,10},{9,11},{10,... | collective-permute-start | bytes 405512 | tf_op jit(solution)/shard_map/ppermute | solution.py:146
  34.9 7.1 %collective-permute-start.10 = (bf16[48,1664]{1,0:T(8,128)(2,1)S(1)}, bf16[48,1664]{1,0:T(8,128)(2,1)S(1)}, u32[]{:S(2)}, u32[]{:S(2)}) collective-permute-start(bf16[48,1664]{1,0:T(8,128)(2,1)S(1)} %broadcast_select_fusion.2), channel_id=1, source_target_pairs={{0,2},{1,3},{2,0},{3,1},{4,6},{5,7},{6,4},{7,5},{8,10},{9,11},{10,... | collective-permute-start | bytes 479240 | tf_op jit(solution)/shard_map/ppermute | solution.py:146
  39.5 7.2 %collective-permute-start.17 = (bf16[192,1408]{1,0:T(8,128)(2,1)S(1)}, bf16[192,1408]{1,0:T(8,128)(2,1)S(1)}, u32[]{:S(2)}, u32[]{:S(2)}) collective-permute-start(bf16[192,1408]{1,0:T(8,128)(2,1)S(1)} %pad_maximum_fusion.1.refs_0_), channel_id=1, source_target_pairs={{0,1},{1,0},{2,3},{3,2},{4,5},{5,4},{6,7},{7,6},{8,9},{9,8},{10,11... | collective-permute-start | bytes 1622024 | tf_op jit(solution)/shard_map/ppermute | solution.py:143
  42.1 9.0 %collective-permute-start.11 = (bf16[192,1664]{1,0:T(8,128)(2,1)S(1)}, bf16[192,1664]{1,0:T(8,128)(2,1)S(1)}, u32[]{:S(2)}, u32[]{:S(2)}) collective-permute-start(bf16[192,1664]{1,0:T(8,128)(2,1)S(1)} %pad_maximum_fusion.refs_0_), channel_id=1, source_target_pairs={{0,1},{1,0},{2,3},{3,2},{4,5},{5,4},{6,7},{7,6},{8,9},{9,8},{10,11... | collective-permute-start | bytes 1916936 | tf_op jit(solution)/shard_map/ppermute | solution.py:143
  42.2 2.3 %collective-permute-start.3 = (bf16[96,1024]{1,0:T(8,128)(2,1)S(1)}, bf16[96,1024]{1,0:T(8,128)(2,1)S(1)}, u32[]{:S(2)}, u32[]{:S(2)}) collective-permute-start(bf16[96,1024]{1,0:T(8,128)(2,1)S(1)} %get-tuple-element.13), channel_id=1, source_target_pairs={{0,1},{1,0},{2,3},{3,2},{4,5},{5,4},{6,7},{7,6},{8,9},{9,8},{10,11... | collective-permute-start | bytes 589832 | tf_op jit(solution)/shard_map/ppermute | solution.py:143
